TPU v7x, 32 devices: a whole 2x2x4 slice. The times are simulated.
32 devices in a mesh: fsdp: 2 (over y), ctx: 4 (over x, core), tp: 4 (over z).
Axes of the slice: x: 2, y: 2, z: 4, core: 2. Of those that a mesh axis runs over, the one named last changes fastest.
Arguments:
- tokens: bfloat16 [4, 2048, 1024], P('fsdp', 'ctx'), may hold values from -6 to 6
- first_values: bfloat16 [4, 2048, 1024], P('fsdp', 'ctx', 'tp'), may hold values from -6 to 6
- norm1_gain: bfloat16 [1024], P('fsdp'), may hold values from 0.5 to 1.5
- norm2_gain: bfloat16 [1024], P('fsdp'), may hold values from 0.5 to 1.5
- w_query: bfloat16 [1024, 1024], P('fsdp', 'tp'), may hold values from -0.1875 to 0.1875
- w_key: bfloat16 [1024, 1024], P('fsdp', 'tp'), may hold values from -0.1875 to 0.1875
- w_value: bfloat16 [1024, 1024], P('fsdp', 'tp'), may hold values from -0.1875 to 0.1875
- w_out: bfloat16 [1024, 1024], P('tp', 'fsdp'), may hold values from -2 to 2
- w_gate: bfloat16 [1024, 2816], P('fsdp', 'tp'), may hold values from -0.1875 to 0.1875
- w_up: bfloat16 [1024, 2816], P('fsdp', 'tp'), may hold values from -0.1875 to 0.1875
- w_down: bfloat16 [2816, 1024], P('tp', 'fsdp'), may hold values from -0.109375 to 0.109375
- prefix: int32 [4], P('fsdp'), may hold values from 204 to 1024
- cotangent: bfloat16 [4, 2048, 1024], P('fsdp', 'ctx'), may hold values from -6 to 6
Outputs:
- block_out: bfloat16 [4, 2048, 1024], P('fsdp', 'ctx')
- token_grad: float32 [4, 2048, 1024], P('fsdp', 'ctx')
- first_values_grad: float32 [4, 2048, 1024], P('fsdp', 'ctx', 'tp')
- norm1_gain_grad: float32 [1024], P('fsdp')
- norm2_gain_grad: float32 [1024], P('fsdp')
- w_query_grad: float32 [1024, 1024], P('fsdp', 'tp')
- w_key_grad: float32 [1024, 1024], P('fsdp', 'tp')
- w_value_grad: float32 [1024, 1024], P('fsdp', 'tp')
- w_out_grad: float32 [1024, 1024], P('tp', 'fsdp')
- w_gate_grad: float32 [1024, 2816], P('fsdp', 'tp')
- w_up_grad: float32 [1024, 2816], P('fsdp', 'tp')
- w_down_grad: float32 [2816, 1024], P('tp', 'fsdp')
All inputs are finite; a program needn't handle non-finite values.
Results may differ from a plain program's by a relative error of at most 0.023.
Values may be sent and summed in bfloat16 or wider, within the bound.
A program may use at most 128 MiB of HBM per device.

v0:
```python
import jax
import jax.numpy as jnp
from jax import lax
from jax.sharding import PartitionSpec as P

HEAD_DIM = 64


epsilon = 1e-06
rope_base = 10000.0
masked_score = -1e30


def passed_along(block, axis, distance):
    devices = range(lax.axis_size(axis))
    route = [((i - distance) % len(devices), i) for i in devices]
    return lax.ppermute(block, axis, route)


def rms_scale(values, gain_vector):
    return (
        values
        * lax.rsqrt(jnp.mean(values * values, axis=-1, keepdims=True) + epsilon)
        * gain_vector
    )


def rms_back(values, gain_vector, upstream):
    factor = lax.rsqrt(jnp.mean(values * values, axis=-1, keepdims=True) + epsilon)
    scaled = upstream * gain_vector
    input_grad = factor * scaled - values * factor**3 * jnp.mean(
        scaled * values, axis=-1, keepdims=True
    )
    gain_grad = jnp.sum(upstream * values * factor, axis=(0, 1))
    return (input_grad, gain_grad)


def rope_tables(positions):
    half_dim = HEAD_DIM // 2
    frequency = rope_base ** (-jnp.arange(half_dim, dtype=jnp.float32) / half_dim)
    angles = positions.astype(jnp.float32)[:, None] * frequency[None, :]
    angles = jnp.concatenate([angles, angles], axis=1)
    return (jnp.cos(angles), jnp.sin(angles))


def rotate(values, cosine_table, sine_table):
    half_dim = values.shape[-1] // 2
    turned = jnp.concatenate([-values[..., half_dim:], values[..., :half_dim]], axis=-1)
    return values * cosine_table[:, None, :] + turned * sine_table[:, None, :]


def rotate_back(values, cosine_table, sine_table):
    half_dim = values.shape[-1] // 2
    scaled = values * sine_table[:, None, :]
    turned = jnp.concatenate([scaled[..., half_dim:], -scaled[..., :half_dim]], axis=-1)
    return values * cosine_table[:, None, :] + turned


def contract(left_side, right_side):
    return jnp.einsum("sra,srb->ab", left_side, right_side, preferred_element_type=jnp.float32)


def score_block(query_low, key_low, query_pos, key_pos, limits):
    scores = jnp.einsum(
        "sqhd,skhd->shqk", query_low, key_low, preferred_element_type=jnp.float32
    ) * HEAD_DIM ** (-0.5)
    allowed = (key_pos[None, None, :] <= query_pos[None, :, None]) | (
        key_pos[None, None, :] < limits[:, None, None]
    )
    return (scores, allowed[:, None])


def shards(
    tokens,
    first_values,
    norm1_gain,
    norm2_gain,
    w_query,
    w_key,
    w_value,
    w_out,
    w_gate,
    w_up,
    w_down,
    prefix,
    cotangent,
):
    gathered = (
        lax.all_gather(norm1_gain, "fsdp", axis=0, tiled=True),
        lax.all_gather(norm2_gain, "fsdp", axis=0, tiled=True),
        lax.all_gather(w_query, "fsdp", axis=0, tiled=True),
        lax.all_gather(w_key, "fsdp", axis=0, tiled=True),
        lax.all_gather(w_value, "fsdp", axis=0, tiled=True),
        lax.all_gather(w_out, "fsdp", axis=1, tiled=True),
        lax.all_gather(w_gate, "fsdp", axis=0, tiled=True),
        lax.all_gather(w_up, "fsdp", axis=0, tiled=True),
        lax.all_gather(w_down, "fsdp", axis=1, tiled=True),
    )
    (
        gain_one,
        gain_two,
        full_query,
        full_key,
        full_value,
        full_out,
        full_gate,
        full_up,
        full_down,
    ) = gathered
    seq_count, local_rows = (tokens.shape[0], tokens.shape[1])
    cycle_size = lax.axis_size("ctx")
    my_place = lax.axis_index("ctx")
    local_width = full_query.shape[1]
    head_count = local_width // HEAD_DIM
    shape_four = (seq_count, local_rows, head_count, HEAD_DIM)
    score_scale = HEAD_DIM ** (-0.5)
    positions = my_place * local_rows + jnp.arange(local_rows, dtype=jnp.int32)
    cosine_table, sine_table = rope_tables(positions)
    state_in = tokens.astype(jnp.float32)
    normed_one = rms_scale(state_in, gain_one).astype(jnp.bfloat16)
    query_raw = jnp.dot(normed_one, full_query, preferred_element_type=jnp.float32)
    key_raw = jnp.dot(normed_one, full_key, preferred_element_type=jnp.float32)
    value_raw = jnp.dot(normed_one, full_value, preferred_element_type=jnp.float32)
    query_low = rotate(query_raw.reshape(shape_four), cosine_table, sine_table).astype(jnp.bfloat16)
    key_low = rotate(key_raw.reshape(shape_four), cosine_table, sine_table).astype(jnp.bfloat16)
    value_low = (
        (0.5 * value_raw + 0.5 * first_values.astype(jnp.float32))
        .astype(jnp.bfloat16)
        .reshape(shape_four)
    )

    def absorb(softmax_state, key_pair, source):
        running_max, running_sum, weighted = softmax_state
        key_pos = source * local_rows + jnp.arange(local_rows, dtype=jnp.int32)
        scores, allowed = score_block(query_low, key_pair[0], positions, key_pos, prefix)
        new_max = jnp.maximum(
            running_max, jnp.max(jnp.where(allowed, scores, masked_score), axis=-1)
        )
        weights = jnp.where(allowed, jnp.exp(scores - new_max[..., None]), 0.0)
        fading = jnp.exp(running_max - new_max)
        running_sum = running_sum * fading + jnp.sum(weights, axis=-1)
        weighted = weighted * fading[..., None] + jnp.einsum(
            "shqk,skhd->shqd",
            weights.astype(jnp.bfloat16),
            key_pair[1],
            preferred_element_type=jnp.float32,
        )
        return (new_max, running_sum, weighted)

    def visit_block(softmax_state, key_pair, source):
        result_state = absorb(softmax_state, key_pair, source)
        return result_state

    stat_shape = (seq_count, head_count, local_rows)
    start_state = (
        jnp.full(stat_shape, masked_score, jnp.float32),
        jnp.zeros(stat_shape, jnp.float32),
        jnp.zeros(stat_shape + (HEAD_DIM,), jnp.float32),
    )
    key_pair_start = jnp.stack((key_low, value_low))

    def forward_turn(step_index, loop_carry):
        softmax_state, key_pair = loop_carry
        softmax_state = visit_block(softmax_state, key_pair, (my_place - step_index) % cycle_size)
        key_pair = passed_along(key_pair, "ctx", 1)
        return (softmax_state, key_pair)

    softmax_state, last_pair = lax.fori_loop(
        0, cycle_size - 1, forward_turn, (start_state, key_pair_start)
    )
    running_max, running_sum, weighted = visit_block(
        softmax_state, last_pair, (my_place - cycle_size + 1) % cycle_size
    )
    log_total = running_max + jnp.log(running_sum)
    context = jnp.swapaxes(weighted / running_sum[..., None], 1, 2)
    context_low = context.astype(jnp.bfloat16).reshape(seq_count, local_rows, local_width)
    attn_part = jnp.dot(context_low, full_out, preferred_element_type=jnp.float32)
    hidden_state = state_in + lax.psum(attn_part.astype(jnp.bfloat16), "tp").astype(jnp.float32)
    normed_two = rms_scale(hidden_state, gain_two).astype(jnp.bfloat16)
    gate_value = jnp.dot(normed_two, full_gate, preferred_element_type=jnp.float32)
    up_value = jnp.dot(normed_two, full_up, preferred_element_type=jnp.float32)
    sigmoid_gate = jax.nn.sigmoid(gate_value)
    swish_gate = gate_value * sigmoid_gate
    inner_low = (swish_gate * up_value).astype(jnp.bfloat16)
    ffn_part = jnp.dot(inner_low, full_down, preferred_element_type=jnp.float32)
    block_out = (
        hidden_state + lax.psum(ffn_part.astype(jnp.bfloat16), "tp").astype(jnp.float32)
    ).astype(jnp.bfloat16)
    back_weights = (
        lax.all_gather(norm1_gain, "fsdp", axis=0, tiled=True),
        lax.all_gather(norm2_gain, "fsdp", axis=0, tiled=True),
        lax.all_gather(w_query, "fsdp", axis=0, tiled=True),
        lax.all_gather(w_key, "fsdp", axis=0, tiled=True),
        lax.all_gather(w_value, "fsdp", axis=0, tiled=True),
        lax.all_gather(w_out, "fsdp", axis=1, tiled=True),
        lax.all_gather(w_gate, "fsdp", axis=0, tiled=True),
        lax.all_gather(w_up, "fsdp", axis=0, tiled=True),
        lax.all_gather(w_down, "fsdp", axis=1, tiled=True),
    )
    back_query, back_key, back_value, back_out, back_gate, back_up, back_down = back_weights[2:]
    inner_grad = jnp.einsum("sre,fe->srf", cotangent, back_down, preferred_element_type=jnp.float32)
    gate_grad = (
        inner_grad * up_value * sigmoid_gate * (1.0 + gate_value * (1.0 - sigmoid_gate))
    ).astype(jnp.bfloat16)
    up_grad = (inner_grad * swish_gate).astype(jnp.bfloat16)
    down_weight_grad = contract(inner_low, cotangent)
    gate_weight_grad = contract(normed_two, gate_grad)
    up_weight_grad = contract(normed_two, up_grad)
    normed_two_part = jnp.einsum(
        "srf,ef->sre", gate_grad, back_gate, preferred_element_type=jnp.float32
    ) + jnp.einsum("srf,ef->sre", up_grad, back_up, preferred_element_type=jnp.float32)
    normed_two_grad = lax.psum(normed_two_part.astype(jnp.bfloat16), "tp").astype(jnp.float32)
    back_two, gain_two_grad = rms_back(hidden_state, gain_two, normed_two_grad)
    hidden_grad = cotangent.astype(jnp.float32) + back_two
    branch_low = hidden_grad.astype(jnp.bfloat16)
    out_weight_grad = contract(context_low, branch_low)
    context_grad = (
        jnp.einsum("sre,ce->src", branch_low, back_out, preferred_element_type=jnp.float32)
        .astype(jnp.bfloat16)
        .reshape(shape_four)
    )
    row_delta = jnp.swapaxes(jnp.sum(context_grad.astype(jnp.float32) * context, axis=-1), 1, 2)

    def absorb_back(gradients, key_pair, source):
        query_grad, pair_grad = gradients
        key_pos = source * local_rows + jnp.arange(local_rows, dtype=jnp.int32)
        scores, allowed = score_block(query_low, key_pair[0], positions, key_pos, prefix)
        probability = jnp.where(allowed, jnp.exp(scores - log_total[..., None]), 0.0)
        value_grad = jnp.einsum(
            "shqk,sqhd->skhd",
            probability.astype(jnp.bfloat16),
            context_grad,
            preferred_element_type=jnp.float32,
        )
        prob_grad = jnp.einsum(
            "sqhd,skhd->shqk", context_grad, key_pair[1], preferred_element_type=jnp.float32
        )
        score_grad = (probability * (prob_grad - row_delta[..., None])).astype(jnp.bfloat16)
        query_grad = (
            query_grad
            + jnp.einsum(
                "shqk,skhd->sqhd", score_grad, key_pair[0], preferred_element_type=jnp.float32
            )
            * score_scale
        )
        key_grad = (
            jnp.einsum("shqk,sqhd->skhd", score_grad, query_low, preferred_element_type=jnp.float32)
            * score_scale
        )
        return (query_grad, pair_grad + jnp.stack((key_grad, value_grad)))

    def visit_back(gradients, key_pair, source):
        result_grads = absorb_back(gradients, key_pair, source)
        return result_grads

    def backward_turn(step_index, loop_carry):
        gradients, key_pair = loop_carry
        gradients = visit_back(gradients, key_pair, (my_place - step_index) % cycle_size)
        key_pair = passed_along(key_pair, "ctx", 1)
        moved_grads = passed_along(gradients[1].astype(jnp.bfloat16), "ctx", 1).astype(jnp.float32)
        return ((gradients[0], moved_grads), key_pair)

    grads_start = (jnp.zeros(shape_four, jnp.float32), jnp.zeros((2,) + shape_four, jnp.float32))
    gradients, returned_pair = lax.fori_loop(
        0, cycle_size, backward_turn, (grads_start, key_pair_start)
    )
    query_grad = gradients[0]
    key_grad = gradients[1][0]
    value_grad = gradients[1][1]
    flat_shape = (seq_count, local_rows, local_width)
    query_proj_grad = (
        rotate_back(query_grad, cosine_table, sine_table).astype(jnp.bfloat16).reshape(flat_shape)
    )
    key_proj_grad = (
        rotate_back(key_grad, cosine_table, sine_table).astype(jnp.bfloat16).reshape(flat_shape)
    )
    half_value_grad = (0.5 * value_grad).reshape(flat_shape)
    value_proj_grad = half_value_grad.astype(jnp.bfloat16)
    query_weight_grad = contract(normed_one, query_proj_grad)
    key_weight_grad = contract(normed_one, key_proj_grad)
    value_weight_grad = contract(normed_one, value_proj_grad)
    normed_one_part = jnp.einsum(
        "src,ec->sre", query_proj_grad, back_query, preferred_element_type=jnp.float32
    )
    normed_one_part = normed_one_part + jnp.einsum(
        "src,ec->sre", key_proj_grad, back_key, preferred_element_type=jnp.float32
    )
    normed_one_part = normed_one_part + jnp.einsum(
        "src,ec->sre", value_proj_grad, back_value, preferred_element_type=jnp.float32
    )
    normed_one_grad = lax.psum(normed_one_part.astype(jnp.bfloat16), "tp").astype(jnp.float32)
    back_one, gain_one_grad = rms_back(state_in, gain_one, normed_one_grad)
    token_grad = hidden_grad + back_one
    shard_sums = (
        lax.psum_scatter(
            gain_one_grad.astype(jnp.bfloat16), "fsdp", scatter_dimension=0, tiled=True
        ).astype(jnp.float32),
        lax.psum_scatter(
            gain_two_grad.astype(jnp.bfloat16), "fsdp", scatter_dimension=0, tiled=True
        ).astype(jnp.float32),
        lax.psum_scatter(
            query_weight_grad.astype(jnp.bfloat16), "fsdp", scatter_dimension=0, tiled=True
        ).astype(jnp.float32),
        lax.psum_scatter(
            key_weight_grad.astype(jnp.bfloat16), "fsdp", scatter_dimension=0, tiled=True
        ).astype(jnp.float32),
        lax.psum_scatter(
            value_weight_grad.astype(jnp.bfloat16), "fsdp", scatter_dimension=0, tiled=True
        ).astype(jnp.float32),
        lax.psum_scatter(
            out_weight_grad.astype(jnp.bfloat16), "fsdp", scatter_dimension=1, tiled=True
        ).astype(jnp.float32),
        lax.psum_scatter(
            gate_weight_grad.astype(jnp.bfloat16), "fsdp", scatter_dimension=0, tiled=True
        ).astype(jnp.float32),
        lax.psum_scatter(
            up_weight_grad.astype(jnp.bfloat16), "fsdp", scatter_dimension=0, tiled=True
        ).astype(jnp.float32),
        lax.psum_scatter(
            down_weight_grad.astype(jnp.bfloat16), "fsdp", scatter_dimension=1, tiled=True
        ).astype(jnp.float32),
    )
    sum_one, sum_two, sum_query, sum_key, sum_value, sum_out, sum_gate, sum_up, sum_down = (
        shard_sums
    )
    totals = (
        lax.psum(sum_one.astype(jnp.bfloat16), "ctx").astype(jnp.float32),
        lax.psum(sum_two.astype(jnp.bfloat16), "ctx").astype(jnp.float32),
        lax.psum(sum_query.astype(jnp.bfloat16), "ctx").astype(jnp.float32),
        lax.psum(sum_key.astype(jnp.bfloat16), "ctx").astype(jnp.float32),
        lax.psum(sum_value.astype(jnp.bfloat16), "ctx").astype(jnp.float32),
        lax.psum(sum_out.astype(jnp.bfloat16), "ctx").astype(jnp.float32),
        lax.psum(sum_gate.astype(jnp.bfloat16), "ctx").astype(jnp.float32),
        lax.psum(sum_up.astype(jnp.bfloat16), "ctx").astype(jnp.float32),
        lax.psum(sum_down.astype(jnp.bfloat16), "ctx").astype(jnp.float32),
    )
    return (
        block_out,
        token_grad,
        half_value_grad,
        totals[0],
        totals[1],
        totals[2],
        totals[3],
        totals[4],
        totals[5],
        totals[6],
        totals[7],
        totals[8],
    )


def solution(mesh):
    return jax.shard_map(
        shards,
        mesh=mesh,
        in_specs=(
            P("fsdp", "ctx", None),
            P("fsdp", "ctx", "tp"),
            P("fsdp"),
            P("fsdp"),
            P("fsdp", "tp"),
            P("fsdp", "tp"),
            P("fsdp", "tp"),
            P("tp", "fsdp"),
            P("fsdp", "tp"),
            P("fsdp", "tp"),
            P("tp", "fsdp"),
            P("fsdp"),
            P("fsdp", "ctx", None),
        ),
        out_specs=(
            P("fsdp", "ctx", None),
            P("fsdp", "ctx", None),
            P("fsdp", "ctx", "tp"),
            P("fsdp"),
            P("fsdp"),
            P("fsdp", "tp"),
            P("fsdp", "tp"),
            P("fsdp", "tp"),
            P("tp", "fsdp"),
            P("fsdp", "tp"),
            P("fsdp", "tp"),
            P("tp", "fsdp"),
        ),
        check_vma=False,
    )
```

profile of v0, /device:TPU:0, one launch (start us, length us, event | category | flops | bytes accessed | tf_op | source)
XLA Modules:
  0.0 822.4 jit_solution(7373627294109482244)
XLA Ops:
  8.8 5.2 all-gather
  20.0 8.1 all_gather.37
  30.1 8.7 %all_gather.35 = bf16[1024,256]{0,1:T(8,128)(2,1)} all-gather(bf16[512,256]{0,1:T(8,128)(2,1)} %copy.65), channel_id=1, replica_groups=mesh['fsdp'=2,'ctx'=4,'tp'=4] {'fsdp'}, dimensions={0}, use_global_device_ids=true | all-gather | bytes 786432 | tf_op jit(solution)/shard_map/all_gather | solution.py:92
  40.6 7.5 all_gather.36
  48.1 8.5 %all_gather.38 = bf16[256,1024]{1,0:T(8,128)(2,1)} all-gather(bf16[256,512]{1,0:T(8,128)(2,1)} %param.24), channel_id=1, replica_groups=mesh['fsdp'=2,'ctx'=4,'tp'=4] {'fsdp'}, dimensions={1}, use_global_device_ids=true | all-gather | bytes 786432 | tf_op jit(solution)/shard_map/all_gather | solution.py:94
  65.5 54.3 %while.42 = (s32[]{:T(128)}, f32[2,4,512]{2,1,0:T(4,128)S(1)}, f32[2,4,512]{2,1,0:T(4,128)S(1)}, f32[2,4,512,64]{2,3,1,0:T(8,128)}, bf16[2,2,512,4,64]{2,4,3,1,0...) while((s32[]{:T(128)}, f32[2,4,512]{2,1,0:T(4,128)S(1)}, ...), condition=%wide.region_4.5_spmd.clone, body=%wide.region_1.4_spmd.clone.sunk | while | flops 561534976 | bytes 71577960 | solution.py:168
  76.8 6.5 fusion.179
  95.7 6.7 fusion.179
  113.1 6.7 fusion.179
  137.8 80.9 %all-reduce.11.cloned.1.call-done = bf16[2,512,1024]{2,1,0:T(8,128)(2,1)} async-done(((bf16[2,512,1024]{2,1,0:T(8,128)(2,1)}), bf16[2,512,1024]{2,1,0:T(8,128)(2,1)}) %all-reduce.11.cloned.1.call-update) | async-done | bytes 2097168 | tf_op jit(solution)/shard_map/psum | solution.py:178
  223.3 5.2 fusion.67
  228.6 5.3 fusion.71
  233.8 7.6 multiply_convert_fusion.2
  265.1 67.6 %all-reduce.13.cloned.1.call-done = bf16[2,512,1024]{2,1,0:T(8,128)(2,1)} async-done(((bf16[2,512,1024]{2,1,0:T(8,128)(2,1)}), bf16[2,512,1024]{2,1,0:T(8,128)(2,1)}) %all-reduce.13.cloned.1.call-update) | async-done | bytes 2097168 | tf_op jit(solution)/shard_map/psum | solution.py:212
  341.6 152.2 %while.43 = (s32[]{:T(128)}, f32[2,512,4,64]{1,3,2,0:T(8,128)}, f32[2,2,512,4,64]{2,4,3,1,0:T(8,128)}, bf16[2,2,512,4,64]{2,4,3,1,0:T(8,128)(2,1)S(1)}, s32[]{:T...) while((s32[]{:T(128)}, f32[2,512,4,64]{1,3,2,0:T(8,128)}, ...), condition=%wide.region_14.15_spmd.clone, body=%wide.region_13.14_spmd.clone.sunk | while | flops 1367607296 | bytes 93909456 | solution.py:264
  360.1 8.4 %collective-permute-done.1 = bf16[2,2,512,4,64]{2,4,3,1,0:T(8,128)(2,1)} collective-permute-done((bf16[2,2,512,4,64]{2,4,3,1,0:T(8,128)(2,1)}, bf16[2,2,512,4,64]{2,4,3,1,0:T(8,128)(2,1)}, u32[]{:S(2)}, u32[]{:S(2)}) %collective-permute-start.1) | collective-permute-done | bytes 1048608 | tf_op jit(solution)/shard_map/while/body/eval_jaxpr/ppermute | solution.py:17
  371.4 8.3 %collective-permute-done.2 = bf16[2,2,512,4,64]{2,4,3,1,0:T(8,128)(2,1)S(1)} collective-permute-done((bf16[2,2,512,4,64]{2,4,3,1,0:T(8,128)(2,1)S(1)}, bf16[2,2,512,4,64]{2,4,3,1,0:T(8,128)(2,1)S(1)}, u32[]{:S(2)}, u32[]{:S(2)}) %collective-permute-start.2) | collective-permute-done | bytes 1048608 | tf_op jit(solution)/shard_map/while/body/eval_jaxpr/ppermute | solution.py:17
  398.5 8.1 collective-permute-done.1
  409.4 8.3 %collective-permute-done.2 = bf16[2,2,512,4,64]{2,4,3,1,0:T(8,128)(2,1)S(1)} collective-permute-done((bf16[2,2,512,4,64]{2,4,3,1,0:T(8,128)(2,1)S(1)}, bf16[2,2,512,4,64]{2,4,3,1,0:T(8,128)(2,1)S(1)}, u32[]{:S(2)}, u32[]{:S(2)}) %collective-permute-start.2) | collective-permute-done | bytes 1048608 | tf_op jit(solution)/shard_map/while/body/eval_jaxpr/ppermute | solution.py:17
  436.5 8.1 collective-permute-done.1
  447.5 8.3 %collective-permute-done.2 = bf16[2,2,512,4,64]{2,4,3,1,0:T(8,128)(2,1)S(1)} collective-permute-done((bf16[2,2,512,4,64]{2,4,3,1,0:T(8,128)(2,1)S(1)}, bf16[2,2,512,4,64]{2,4,3,1,0:T(8,128)(2,1)S(1)}, u32[]{:S(2)}, u32[]{:S(2)}) %collective-permute-start.2) | collective-permute-done | bytes 1048608 | tf_op jit(solution)/shard_map/while/body/eval_jaxpr/ppermute | solution.py:17
  474.6 8.1 collective-permute-done.1
  485.5 8.3 %collective-permute-done.2 = bf16[2,2,512,4,64]{2,4,3,1,0:T(8,128)(2,1)S(1)} collective-permute-done((bf16[2,2,512,4,64]{2,4,3,1,0:T(8,128)(2,1)S(1)}, bf16[2,2,512,4,64]{2,4,3,1,0:T(8,128)(2,1)S(1)}, u32[]{:S(2)}, u32[]{:S(2)}) %collective-permute-start.2) | collective-permute-done | bytes 1048608 | tf_op jit(solution)/shard_map/while/body/eval_jaxpr/ppermute | solution.py:17
  518.2 11.0 %reduce-scatter.10.cloned.1.call-done = bf16[512,256]{1,0:T(8,128)(2,1)} async-done(((bf16[1024,256]{1,0:T(8,128)(2,1)}), bf16[512,256]{1,0:T(8,128)(2,1)}) %reduce-scatter.10.cloned.1.call-update) | async-done | bytes 262160 | tf_op jit(solution)/shard_map/reduce_scatter | solution.py:304
  529.1 16.7 %reduce-scatter.12.cloned.1.call-done = bf16[512,256]{1,0:T(8,128)(2,1)} async-done(((bf16[1024,256]{1,0:T(8,128)(2,1)}), bf16[512,256]{1,0:T(8,128)(2,1)}) %reduce-scatter.12.cloned.1.call-update) | async-done | bytes 262160 | tf_op jit(solution)/shard_map/reduce_scatter | solution.py:307
  545.8 17.3 %reduce-scatter.8.cloned.1.call-done = bf16[512,256]{1,0:T(8,128)(2,1)} async-done(((bf16[1024,256]{1,0:T(8,128)(2,1)}), bf16[512,256]{1,0:T(8,128)(2,1)}) %reduce-scatter.8.cloned.1.call-update) | async-done | bytes 262160 | tf_op jit(solution)/shard_map/reduce_scatter | solution.py:301
  563.3 5.0 convolution_convert_fusion.1
  574.4 59.6 %all-reduce.17.cloned.1.call-done = (bf16[512,256]{1,0:T(8,128)(2,1)}, bf16[512,256]{1,0:T(8,128)(2,1)}, bf16[512,256]{1,0:T(8,128)(2,1)}, bf16[256,512]{1,0:T(8...) async-done(((bf16[512,256]{1,0:T(8,128)(2,1)}, bf16[512,256]{1,0:T(8,128)(2,1)}, bf16[512,256]{1,0:T(8,128)(2,1)}, ...) | async-done | bytes 3211280 | tf_op jit(solution)/shard_map/psum | solution.py:329
  646.3 146.1 %all-reduce.15.cloned.1.call-done = (bf16[2,512,1024]{2,1,0:T(8,128)(2,1)}, bf16[2,512,1024]{2,1,0:T(8,128)(2,1)}) async-done(((bf16[2,512,1024]{2,1,0:T(8,128)(2,1)}, bf16[2,512,1024]{2,1,0:T(8,128)(2,1)}), (bf16[2,512,1024]{2,1,0:T(8,128)(2,1)}, bf16[2,512,1024]{2,1,0:T(8,128)(2,1)})) %all-reduce.15.cloned.1.call-update) | async-done | bytes 4194320 | tf_op jit(solution)/shard_map/psum | solution.py:187
  795.8 4.9 all-reduce.5
  800.9 5.6 all-reduce.3
  807.7 7.4 fusion.46
  (338 shorter events, 240.3 us)
Async XLA Ops:
  8.0 210.7 %all-reduce.11.cloned.1.call-start = ((), (), s32[]{:S(2)}) async-start(), calls=%async_computation.7 | async-start | bytes 4194304 | tf_op jit(solution)/shard_map/psum | solution.py:178
  14.1 47.6 %copy-start.39 = (f32[2,1,512]{2,1,0:T(1,128)}, f32[2,1,512]{2,1,0:T(1,128)S(1)}, u32[]{:S(2)}) copy-start(f32[2,1,512]{2,1,0:T(1,128)S(1)} %convert_element_type.278) | copy-start | bytes 12292
  14.1 44.6 %copy-start.2 = (bf16[2,512,1024]{2,1,0:T(8,128)(2,1)S(1)}, bf16[2,512,1024]{2,1,0:T(8,128)(2,1)}, u32[]{:S(2)}) copy-start(bf16[2,512,1024]{2,1,0:T(8,128)(2,1)} %param.17) | copy-start | bytes 6291460
  16.9 44.7 %copy-start.37 = (f32[2,512]{1,0:T(2,128)}, f32[2,512]{1,0:T(2,128)S(1)}, u32[]{:S(2)}) copy-start(f32[2,512]{1,0:T(2,128)S(1)} %get-tuple-element.688) | copy-start | bytes 12292
  17.3 48.0 %copy-start.18 = (f32[512,64]{0,1:T(8,128)}, f32[512,64]{0,1:T(8,128)S(1)}, u32[]{:S(2)}) copy-start(f32[512,64]{0,1:T(8,128)S(1)} %get-tuple-element.686) | copy-start | bytes 393220
  28.2 32.4 %copy-start.20 = (bf16[1024,256]{0,1:T(8,128)(2,1)}, bf16[1024,256]{0,1:T(8,128)(2,1)S(1)}, u32[]{:S(2)}) copy-start(bf16[1024,256]{0,1:T(8,128)(2,1)S(1)} %all_gather.37) | copy-start | bytes 1572868
  68.3 15.0 %collective-permute-start = (bf16[2,2,512,4,64]{2,4,3,1,0:T(8,128)(2,1)}, bf16[2,2,512,4,64]{2,4,3,1,0:T(8,128)(2,1)}, u32[]{:S(2)}, u32[]{:S(2)}) collective-permute-start(bf16[2,2,512,4,64]{2,4,3,1,0:T(8,128)(2,1)} %copy.107), channel_id=1, source_target_pairs={{12,0},{0,4},{4,8},{8,12},{13,1},{1,5},{5,9},{9,13},{14,2},{2,6},{... | collective-permute-start | bytes 3145736 | tf_op jit(solution)/shard_map/while/body/eval_jaxpr/ppermute | solution.py:17
  85.6 16.8 %collective-permute-start = (bf16[2,2,512,4,64]{2,4,3,1,0:T(8,128)(2,1)}, bf16[2,2,512,4,64]{2,4,3,1,0:T(8,128)(2,1)}, u32[]{:S(2)}, u32[]{:S(2)}) collective-permute-start(bf16[2,2,512,4,64]{2,4,3,1,0:T(8,128)(2,1)} %copy.107), channel_id=1, source_target_pairs={{12,0},{0,4},{4,8},{8,12},{13,1},{1,5},{5,9},{9,13},{14,2},{2,6},{... | collective-permute-start | bytes 3145736 | tf_op jit(solution)/shard_map/while/body/eval_jaxpr/ppermute | solution.py:17
  104.6 15.2 %collective-permute-start = (bf16[2,2,512,4,64]{2,4,3,1,0:T(8,128)(2,1)}, bf16[2,2,512,4,64]{2,4,3,1,0:T(8,128)(2,1)}, u32[]{:S(2)}, u32[]{:S(2)}) collective-permute-start(bf16[2,2,512,4,64]{2,4,3,1,0:T(8,128)(2,1)} %copy.107), channel_id=1, source_target_pairs={{12,0},{0,4},{4,8},{8,12},{13,1},{1,5},{5,9},{9,13},{14,2},{2,6},{... | collective-permute-start | bytes 3145736 | tf_op jit(solution)/shard_map/while/body/eval_jaxpr/ppermute | solution.py:17
  131.5 91.9 %all-gather.8.cloned.1.call-start = ((), (), s32[]{:S(2)}) async-start(), calls=%async_computation.9 | async-start | bytes 2162688 | tf_op jit(solution)/shard_map/all_gather | solution.py:96
  132.0 96.5 %all-gather.6.cloned.1.call-start = ((), (), s32[]{:S(2)}) async-start(), calls=%async_computation.8 | async-start | bytes 2162688 | tf_op jit(solution)/shard_map/all_gather | solution.py:95
  132.6 101.2 %all-gather.10.cloned.1.call-start = ((), (), s32[]{:S(2)}) async-start(), calls=%async_computation.10 | async-start | bytes 2162688 | tf_op jit(solution)/shard_map/all_gather | solution.py:97
  133.2 199.5 %all-reduce.13.cloned.1.call-start = ((), (), s32[]{:S(2)}) async-start(), calls=%async_computation.11 | async-start | bytes 4194304 | tf_op jit(solution)/shard_map/psum | solution.py:212
  247.1 271.0 %reduce-scatter.20.cloned.1.call-start = ((), (), s32[]{:S(2)}) async-start(), calls=%async_computation.18 | async-start | bytes 2162688 | tf_op jit(solution)/shard_map/reduce_scatter | solution.py:319
  252.0 266.1 %reduce-scatter.16.cloned.1.call-start = ((), (), s32[]{:S(2)}) async-start(), calls=%async_computation.16 | async-start | bytes 2162688 | tf_op jit(solution)/shard_map/reduce_scatter | solution.py:313
  256.9 261.3 %reduce-scatter.18.cloned.1.call-start = ((), (), s32[]{:S(2)}) async-start(), calls=%async_computation.17 | async-start | bytes 2162688 | tf_op jit(solution)/shard_map/reduce_scatter | solution.py:316
  264.6 253.5 %reduce-scatter.14.cloned.1.call-start = ((), (), s32[]{:S(2)}) async-start(), calls=%async_computation.15 | async-start | bytes 786432 | tf_op jit(solution)/shard_map/reduce_scatter | solution.py:310
  341.6 152.2 %copy-start.19 = (f32[512,64]{0,1:T(8,128)S(1)}, f32[512,64]{0,1:T(8,128)}, u32[]{:S(2)}) copy-start(f32[512,64]{0,1:T(8,128)} %copy-done.18) | copy-start | bytes 393220
  354.0 14.5 %collective-permute-start.1 = (bf16[2,2,512,4,64]{2,4,3,1,0:T(8,128)(2,1)}, bf16[2,2,512,4,64]{2,4,3,1,0:T(8,128)(2,1)}, u32[]{:S(2)}, u32[]{:S(2)}) collective-permute-start(bf16[2,2,512,4,64]{2,4,3,1,0:T(8,128)(2,1)} %fusion.194), channel_id=1, source_target_pairs={{12,0},{0,4},{4,8},{8,12},{13,1},{1,5},{5,9},{9,13},{14,2},{2,6},{... | collective-permute-start | bytes 3145736 | tf_op jit(solution)/shard_map/while/body/eval_jaxpr/ppermute | solution.py:17
  354.0 25.7 %collective-permute-start.2 = (bf16[2,2,512,4,64]{2,4,3,1,0:T(8,128)(2,1)S(1)}, bf16[2,2,512,4,64]{2,4,3,1,0:T(8,128)(2,1)S(1)}, u32[]{:S(2)}, u32[]{:S(2)}) collective-permute-start(bf16[2,2,512,4,64]{2,4,3,1,0:T(8,128)(2,1)S(1)} %copy.122), channel_id=1, source_target_pairs={{12,0},{0,4},{4,8},{8,12},{13,1},{1,5},{5,9},{9,13},{14,2},{2,6},{... | collective-permute-start | bytes 3145736 | tf_op jit(solution)/shard_map/while/body/eval_jaxpr/ppermute | solution.py:17
  392.0 14.5 %collective-permute-start.1 = (bf16[2,2,512,4,64]{2,4,3,1,0:T(8,128)(2,1)}, bf16[2,2,512,4,64]{2,4,3,1,0:T(8,128)(2,1)}, u32[]{:S(2)}, u32[]{:S(2)}) collective-permute-start(bf16[2,2,512,4,64]{2,4,3,1,0:T(8,128)(2,1)} %fusion.194), channel_id=1, source_target_pairs={{12,0},{0,4},{4,8},{8,12},{13,1},{1,5},{5,9},{9,13},{14,2},{2,6},{... | collective-permute-start | bytes 3145736 | tf_op jit(solution)/shard_map/while/body/eval_jaxpr/ppermute | solution.py:17
  392.0 25.7 %collective-permute-start.2 = (bf16[2,2,512,4,64]{2,4,3,1,0:T(8,128)(2,1)S(1)}, bf16[2,2,512,4,64]{2,4,3,1,0:T(8,128)(2,1)S(1)}, u32[]{:S(2)}, u32[]{:S(2)}) collective-permute-start(bf16[2,2,512,4,64]{2,4,3,1,0:T(8,128)(2,1)S(1)} %copy.122), channel_id=1, source_target_pairs={{12,0},{0,4},{4,8},{8,12},{13,1},{1,5},{5,9},{9,13},{14,2},{2,6},{... | collective-permute-start | bytes 3145736 | tf_op jit(solution)/shard_map/while/body/eval_jaxpr/ppermute | solution.py:17
  430.1 14.5 %collective-permute-start.1 = (bf16[2,2,512,4,64]{2,4,3,1,0:T(8,128)(2,1)}, bf16[2,2,512,4,64]{2,4,3,1,0:T(8,128)(2,1)}, u32[]{:S(2)}, u32[]{:S(2)}) collective-permute-start(bf16[2,2,512,4,64]{2,4,3,1,0:T(8,128)(2,1)} %fusion.194), channel_id=1, source_target_pairs={{12,0},{0,4},{4,8},{8,12},{13,1},{1,5},{5,9},{9,13},{14,2},{2,6},{... | collective-permute-start | bytes 3145736 | tf_op jit(solution)/shard_map/while/body/eval_jaxpr/ppermute | solution.py:17
  430.1 25.7 %collective-permute-start.2 = (bf16[2,2,512,4,64]{2,4,3,1,0:T(8,128)(2,1)S(1)}, bf16[2,2,512,4,64]{2,4,3,1,0:T(8,128)(2,1)S(1)}, u32[]{:S(2)}, u32[]{:S(2)}) collective-permute-start(bf16[2,2,512,4,64]{2,4,3,1,0:T(8,128)(2,1)S(1)} %copy.122), channel_id=1, source_target_pairs={{12,0},{0,4},{4,8},{8,12},{13,1},{1,5},{5,9},{9,13},{14,2},{2,6},{... | collective-permute-start | bytes 3145736 | tf_op jit(solution)/shard_map/while/body/eval_jaxpr/ppermute | solution.py:17
  468.1 14.5 %collective-permute-start.1 = (bf16[2,2,512,4,64]{2,4,3,1,0:T(8,128)(2,1)}, bf16[2,2,512,4,64]{2,4,3,1,0:T(8,128)(2,1)}, u32[]{:S(2)}, u32[]{:S(2)}) collective-permute-start(bf16[2,2,512,4,64]{2,4,3,1,0:T(8,128)(2,1)} %fusion.194), channel_id=1, source_target_pairs={{12,0},{0,4},{4,8},{8,12},{13,1},{1,5},{5,9},{9,13},{14,2},{2,6},{... | collective-permute-start | bytes 3145736 | tf_op jit(solution)/shard_map/while/body/eval_jaxpr/ppermute | solution.py:17
  468.2 25.7 %collective-permute-start.2 = (bf16[2,2,512,4,64]{2,4,3,1,0:T(8,128)(2,1)S(1)}, bf16[2,2,512,4,64]{2,4,3,1,0:T(8,128)(2,1)S(1)}, u32[]{:S(2)}, u32[]{:S(2)}) collective-permute-start(bf16[2,2,512,4,64]{2,4,3,1,0:T(8,128)(2,1)S(1)} %copy.122), channel_id=1, source_target_pairs={{12,0},{0,4},{4,8},{8,12},{13,1},{1,5},{5,9},{9,13},{14,2},{2,6},{... | collective-permute-start | bytes 3145736 | tf_op jit(solution)/shard_map/while/body/eval_jaxpr/ppermute | solution.py:17
  498.4 30.7 %reduce-scatter.10.cloned.1.call-start = ((), (), s32[]{:S(2)}) async-start(), calls=%async_computation.13 | async-start | bytes 786432 | tf_op jit(solution)/shard_map/reduce_scatter | solution.py:304
  509.0 36.9 %reduce-scatter.12.cloned.1.call-start = ((), (), s32[]{:S(2)}) async-start(), calls=%async_computation.14 | async-start | bytes 786432 | tf_op jit(solution)/shard_map/reduce_scatter | solution.py:307
  513.7 49.5 %reduce-scatter.8.cloned.1.call-start = ((), (), s32[]{:S(2)}) async-start(), calls=%async_computation.12 | async-start | bytes 786432 | tf_op jit(solution)/shard_map/reduce_scatter | solution.py:301
  518.0 116.0 %all-reduce.17.cloned.1.call-start = ((), (), s32[]{:S(2)}) async-start(), calls=%async_computation.20 | async-start | bytes 6422528 | tf_op jit(solution)/shard_map/psum | solution.py:329
  563.2 229.2 %all-reduce.15.cloned.1.call-start = ((), (), s32[]{:S(2)}) async-start(), calls=%async_computation.19 | async-start | bytes 8388608 | tf_op jit(solution)/shard_map/psum | solution.py:187
  643.7 164.0 %copy-start.41 = (f32[2,512]{1,0:T(2,128)S(1)}, f32[2,512]{1,0:T(2,128)}, u32[]{:S(2)}) copy-start(f32[2,512]{1,0:T(2,128)} %get-tuple-element.687) | copy-start | bytes 12292
  (53 other events, 181.8 us)
Sparse Core Ops, SparseCore 0:
  131.6 87.0 all-reduce.10
  247.2 85.4 all-reduce.12
  563.3 70.6 all-reduce.16
  636.8 155.5 all-reduce.14
Sparse Core Ops, SparseCore 1:
  133.6 26.1 all-gather.7
  161.2 25.5 all-gather.5
  188.3 25.6 all-gather.9
  252.1 23.5 reduce-scatter.19
  278.5 24.5 reduce-scatter.15
  305.9 24.5 reduce-scatter.17
  498.5 13.4 reduce-scatter.13
  514.7 14.4 reduce-scatter.9
  531.3 14.4 reduce-scatter.11
  548.7 14.4 reduce-scatter.7
where the time goes:
time: 829 us; the launch traced here: 822 us
  waiting for transfers between devices  467 us (56%)
  matrix products  147 us (18%)
  other arithmetic  79.4 us (10%)
  blocking collectives  53.2 us (6%)
  local copies, waits for them, and re-layouts  49.2 us (6%)
  between operations  16.9 us (2%)
  starting transfers between devices  9.09 us (1%)
    psum x1, waiting for transfers between devices, shards(): lax.psum(ffn_part.astype(jnp.bfloat16), 'tp').astype(jnp.float32)  146 us
    psum x1, waiting for transfers between devices, shards(): lax.psum(attn_part.astype(jnp.bfloat16), 'tp').astype(jnp.float32)  80.9 us
    psum x1, waiting for transfers between devices, shards(): lax.psum(normed_two_part.astype(jnp.bfloat16), 'tp').astype(jnp.float32)  67.6 us
    ppermute x11, waiting for transfers between devices, passed_along(): return lax.ppermute(block, axis, route)  66 us
    psum x1, waiting for transfers between devices, shards(): lax.psum(sum_query.astype(jnp.bfloat16), 'ctx').astype(jnp.float32)  59.6 us
    while x40, local copies, waits for them, and re-layouts  26.4 us
    dot_general x4, matrix products, absorb(): jnp.einsum('shqk,skhd->shqd', weights.astype(jnp.bfloat16), key_pair[1],...  23.7 us
    dot_general x7, matrix products, contract(): jnp.einsum('sra,srb->ab', left_side, right_side, preferred_element_type=j...  22.7 us
  transfers between devices with their start and end apart: 25, of which 15 were waited for; matrix products, arithmetic and copies ran while one was open for 23% of the time, Pallas kernels for 0%

commit v1 on v0

v1 whole, which is shorter than its diff:
```python
import functools

import jax
import jax.numpy as jnp
from jax import lax
from jax.experimental import pallas as pl
from jax.experimental.pallas import tpu as pltpu
from jax.sharding import PartitionSpec as P

HEAD_DIM = 64
epsilon = 1e-06
rope_base = 10000.0
masked_score = -1e30
MESH = pl.DeviceIdType.MESH
bf16 = jnp.bfloat16
f32 = jnp.float32


def dot(a, b):
    return jnp.dot(a, b, preferred_element_type=f32)


def dot_nt(a, b):
    return lax.dot_general(a, b, (((1,), (1,)), ((), ())), preferred_element_type=f32)


def unit_norm(values):
    return values * lax.rsqrt(jnp.mean(values * values, axis=-1, keepdims=True) + epsilon)


def low_half(shape):
    return lax.rem(lax.broadcasted_iota(jnp.int32, shape, 1), HEAD_DIM) < HEAD_DIM // 2


def turned(values):
    pieces = []
    half = HEAD_DIM // 2
    for at in range(0, values.shape[1], 128):
        piece = values[:, at : at + 128]
        up = pltpu.roll(piece, 128 - half, 1)
        down = pltpu.roll(piece, half, 1)
        pieces.append(jnp.where(low_half(piece.shape), up, down))
    return jnp.concatenate(pieces, axis=1)


class Sum:
    def __init__(self, place, part, inward, across, result, sems):
        self.pair = place + 1 - 2 * lax.rem(place, 2)
        self.middle = 3 - place
        self.inner = (place == 1) | (place == 2)
        self.outer = (place == 0) | (place == 3)
        self.part, self.inward, self.across, self.result = part, inward, across, result
        self.send_one, self.recv_one, self.send_two, self.recv_two = sems

    def copy_in(self, i):
        return pltpu.make_async_remote_copy(
            src_ref=self.part.at[i], dst_ref=self.inward.at[i], send_sem=self.send_one.at[i],
            recv_sem=self.recv_one.at[i], device_id={"tp": self.pair}, device_id_type=MESH)

    def copy_across(self, i):
        return pltpu.make_async_remote_copy(
            src_ref=self.part.at[i], dst_ref=self.across.at[i], send_sem=self.send_two.at[i],
            recv_sem=self.recv_two.at[i], device_id={"tp": self.middle}, device_id_type=MESH)

    def copy_out(self, i):
        return pltpu.make_async_remote_copy(
            src_ref=self.result.at[i], dst_ref=self.result.at[i], send_sem=self.send_one.at[i],
            recv_sem=self.recv_one.at[i], device_id={"tp": self.pair}, device_id_type=MESH)

    def offer(self, i):
        @pl.when(self.outer)
        def _():
            self.copy_in(i).start()

    def take_in(self, i):
        self.copy_in(i).wait_recv()
        self.part[i] = (self.part[i].astype(f32) + self.inward[i].astype(f32)).astype(bf16)
        self.copy_across(i).start()

    def finish(self, i):
        self.copy_across(i).wait_recv()
        self.result[i] = (self.part[i].astype(f32) + self.across[i].astype(f32)).astype(bf16)
        self.copy_out(i).start()

    def step(self, i, done):
        @pl.when(self.inner)
        def _():
            self.take_in(i)

            @pl.when(i > 0)
            def _():
                self.finish(i - 1)
                done(i - 1)

    def close(self, count, done):
        @pl.when(self.inner)
        def _():
            self.finish(count - 1)
            done(count - 1)

            @pl.loop(0, count)
            def _(i):
                self.copy_across(i).wait_send()
                self.copy_out(i).wait_send()

        @pl.when(self.outer)
        def _():
            @pl.loop(0, count)
            def _(i):
                self.copy_out(i).wait_recv()
                done(i)

            @pl.loop(0, count)
            def _(i):
                self.copy_in(i).wait_send()


def greet(place, ring):
    barrier = pltpu.get_barrier_semaphore()
    peers = (
        {"tp": place + 1 - 2 * lax.rem(place, 2)},
        {"tp": 3 - place},
        {"ctx": ring + 1 - 2 * lax.rem(ring, 2)},
        {"ctx": lax.rem(ring + 2, 4)},
    )
    for peer in peers:
        pl.semaphore_signal(barrier, inc=1, device_id=peer, device_id_type=MESH)
    pl.semaphore_wait(barrier, len(peers))


def attend_kernel(
    tok, fv, g1, wq, wk, wv, wo, cosine, sine, prefix,
    sum_hbm, q_out, kv_hbm, ctx_out, lse_out,
    kv, qtm, vt, acct, maxes, totals, part, inward, across, result,
    kv_send, kv_recv, kv_save, send_one, recv_one, send_two, recv_two, save,
):
    place, ring = lax.axis_index("tp"), lax.axis_index("ctx")
    seqs, rows, width = q_out.shape
    heads = width // HEAD_DIM
    tile = 256
    per_seq = part.shape[0] // seqs
    chunk = part.shape[1]
    mate = {"ctx": ring + 1 - 2 * lax.rem(ring, 2)}
    peer = {"ctx": lax.rem(ring + 2, 4)}
    blocks = (ring, ring + 1 - 2 * lax.rem(ring, 2), lax.rem(ring + 2, 4), 3 - ring)
    greet(place, ring)

    def pass_block(s, source, target, device, slot):
        return pltpu.make_async_remote_copy(
            src_ref=kv.at[s, source], dst_ref=kv.at[s, target], send_sem=kv_send.at[s, slot],
            recv_sem=kv_recv.at[s, target], device_id=device, device_id_type=MESH)

    to_mate = lambda s: pass_block(s, 0, 1, mate, 0)
    to_peer = lambda s: pass_block(s, 0, 2, peer, 1)
    onward = lambda s: pass_block(s, 2, 3, mate, 2)

    for s in range(seqs):
        @pl.loop(0, rows // tile)
        def _(t):
            at = pl.ds(pl.multiple_of(t * tile, tile), tile)
            normed = (unit_norm(tok[s, at, :].astype(f32)) * g1[...].astype(f32)).astype(bf16)
            co, si = cosine[at, :], sine[at, :]
            q = dot(normed, wq[...])
            q = (q * co + turned(q) * si) * HEAD_DIM ** (-0.5)
            q_out[s, at, :] = q.astype(bf16)
            qt = jnp.transpose(q)
            owner = lax.broadcasted_iota(jnp.int32, qt.shape, 0) // HEAD_DIM
            for h in range(heads):
                qtm[s, h, :, at] = jnp.where(owner == h, qt, 0.0).astype(bf16)
            k = dot(normed, wk[...])
            kv[s, 0, 0, at, :] = (k * co + turned(k) * si).astype(bf16)
            v = dot(normed, wv[...])
            kv[s, 0, 1, at, :] = (0.5 * v + 0.5 * fv[s, at, :].astype(f32)).astype(bf16)

        to_peer(s).start()
        to_mate(s).start()

    def attend_block(s, j, block, steps=None):
        vt[...] = jnp.transpose(kv[s, j, 1])
        key_pos = block * rows + lax.broadcasted_iota(jnp.int32, (rows, 1), 0)
        query_pos = ring * rows + lax.broadcasted_iota(jnp.int32, (1, rows), 1)
        seen = key_pos < jnp.maximum(query_pos + 1, prefix[s])

        @pl.loop(0, heads)
        def _(h):
            of_head = pl.ds(pl.multiple_of(h * HEAD_DIM, HEAD_DIM), HEAD_DIM)
            scores = jnp.where(seen, dot(kv[s, j, 0], qtm[s, h]), masked_score)
            old = maxes[h]
            new = jnp.maximum(old, jnp.max(scores, axis=0, keepdims=True))
            weights = jnp.exp(scores - new)
            fade = jnp.exp(old - new)
            maxes[h] = new
            totals[h] = totals[h] * fade + jnp.sum(weights, axis=0, keepdims=True)
            acct[of_head, :] = acct[of_head, :] * fade + dot(vt[of_head, :], weights.astype(bf16))
            if steps is not None:
                @pl.when(lax.rem(h, 2) == 1)
                def _():
                    sums.step(steps + h // 2, done)

    def saving(i):
        return pltpu.make_async_copy(result.at[i], sum_hbm.at[i], save.at[i])

    done = lambda i: saving(i).start()
    sums = Sum(place, part, inward, across, result, (send_one, recv_one, send_two, recv_two))

    for s in range(seqs):
        maxes[...] = jnp.full_like(maxes, masked_score)
        totals[...] = jnp.zeros_like(totals)
        acct[...] = jnp.zeros_like(acct)
        attend_block(s, 0, blocks[0], None if s == 0 else (s - 1) * per_seq + 0)
        to_mate(s).wait_recv()
        attend_block(s, 1, blocks[1], None if s == 0 else (s - 1) * per_seq + 2)
        to_peer(s).wait_recv()
        onward(s).start()
        attend_block(s, 2, blocks[2], None if s == 0 else (s - 1) * per_seq + 4)
        onward(s).wait_recv()
        attend_block(s, 3, blocks[3], None if s == 0 else (s - 1) * per_seq + 6)
        pltpu.make_async_copy(kv.at[s], kv_hbm.at[s], kv_save.at[s]).start()
        for h in range(heads):
            lse_out[s, h : h + 1, :] = maxes[h] + jnp.log(totals[h])
            of_head = slice(h * HEAD_DIM, (h + 1) * HEAD_DIM)
            acct[of_head, :] = acct[of_head, :] / totals[h]
        ctx_out[s] = jnp.transpose(acct[...]).astype(bf16)

        @pl.loop(0, per_seq)
        def _(i):
            at = pl.ds(pl.multiple_of(i * chunk, chunk), chunk)
            part[s * per_seq + i] = dot(ctx_out[s, at, :], wo[...]).astype(bf16)
            sums.offer(s * per_seq + i)

    @pl.loop((seqs - 1) * per_seq, seqs * per_seq)
    def _(i):
        sums.step(i, done)

    sums.close(seqs * per_seq, done)
    for s in range(seqs):
        to_mate(s).wait_send()
        to_peer(s).wait_send()
        onward(s).wait_send()
        pltpu.make_async_copy(kv.at[s], kv_hbm.at[s], kv_save.at[s]).wait()

    @pl.loop(0, seqs * per_seq)
    def _(i):
        saving(i).wait()


def attend(tok, fv, g1, wq, wk, wv, wo, cosine, sine, prefix):
    seqs, rows, dim = tok.shape
    width = wq.shape[1]
    heads = width // HEAD_DIM
    chunk = 64
    count = seqs * rows // chunk
    vmem = pl.BlockSpec(memory_space=pltpu.VMEM)
    anyw = pl.BlockSpec(memory_space=pl.ANY)
    dma = pltpu.SemaphoreType.DMA
    lines = pltpu.VMEM((count, chunk, dim), bf16)
    return pl.pallas_call(
        attend_kernel,
        name="attend",
        out_shape=(
            jax.ShapeDtypeStruct((count, chunk, dim), bf16),
            jax.ShapeDtypeStruct((seqs, rows, width), bf16),
            jax.ShapeDtypeStruct((seqs, 4, 2, rows, width), bf16),
            jax.ShapeDtypeStruct((seqs, rows, width), bf16),
            jax.ShapeDtypeStruct((seqs, heads, rows), f32),
        ),
        in_specs=[vmem] * 9 + [pl.BlockSpec(memory_space=pltpu.SMEM)],
        out_specs=(anyw, vmem, anyw, vmem, vmem),
        scratch_shapes=[
            pltpu.VMEM((seqs, 4, 2, rows, width), bf16),
            pltpu.VMEM((seqs, heads, width, rows), bf16),
            pltpu.VMEM((width, rows), bf16),
            pltpu.VMEM((width, rows), f32),
            pltpu.VMEM((heads, 1, rows), f32),
            pltpu.VMEM((heads, 1, rows), f32),
            lines, lines, lines, lines,
            dma((seqs, 3)), dma((seqs, 4)), dma((seqs,)),
            dma((count,)), dma((count,)), dma((count,)), dma((count,)), dma((count,)),
        ],
        compiler_params=pltpu.CompilerParams(
            collective_id=0, has_side_effects=True, vmem_limit_bytes=60 * 1024 * 1024),
        cost_estimate=pl.CostEstimate(flops=8 * 10**9, bytes_accessed=10**7, transcendentals=10**7),
    )(tok, fv, g1, wq, wk, wv, wo, cosine, sine, prefix)


def forward_ffn(normed, w_gate, w_up):
    gate = dot(normed, w_gate)
    up = dot(normed, w_up)
    return gate, up, jax.nn.sigmoid(gate)


def feed_kernel(
    tok, attn, cot, g2, wg, wu, wd,
    mixed_hbm, late_hbm, dwg, dwu, dwd,
    normed_t, inner_t, inner_s, gg, ug, late, part, inward, across, result,
    send_one, recv_one, send_two, recv_two, save, late_save,
):
    place, ring = lax.axis_index("tp"), lax.axis_index("ctx")
    seqs, rows, dim = tok.shape
    chunk = part.shape[1]
    tile = 256
    tiles = seqs * rows // tile
    early = tiles // 2
    per_tile = tile // chunk
    per_seq_tiles = rows // tile
    count = part.shape[0]
    greet(place, ring)
    sums = Sum(place, part, inward, across, result, (send_one, recv_one, send_two, recv_two))

    def saving(i):
        return pltpu.make_async_copy(result.at[i], mixed_hbm.at[i], save.at[i])

    done = lambda i: saving(i).start()

    def saving_late(t):
        return pltpu.make_async_copy(late.at[t], late_hbm.at[t], late_save.at[t])

    @pl.loop(0, tiles)
    def _(t):
        s, at = t // per_seq_tiles, pl.ds(pl.multiple_of(lax.rem(t, per_seq_tiles) * tile, tile), tile)
        flat = pl.ds(pl.multiple_of(t * tile, tile), tile)
        lanes = pl.ds(pl.multiple_of(t * tile, tile), tile)
        step_base = (t - 1) * per_tile

        def step(k):
            @pl.when(t > 0)
            def _():
                sums.step(step_base + k, done)

        hidden = tok[s, at, :].astype(f32) + attn[s, at, :].astype(f32)
        normed_wide = unit_norm(hidden) * g2[...].astype(f32)
        normed = normed_wide.astype(bf16)
        normed_t[:, lanes] = jnp.transpose(normed)
        gate, up, sigmoid = forward_ffn(normed, wg[...], wu[...])
        swish = gate * sigmoid
        inner = (swish * up).astype(bf16)
        inner_s[...] = inner
        inner_t[:, lanes] = jnp.transpose(inner)
        inner_grad = dot_nt(cot[s, at, :], wd[...])
        gg[flat, :] = (inner_grad * up * sigmoid * (1.0 + gate * (1.0 - sigmoid))).astype(bf16)
        ug[flat, :] = (inner_grad * swish).astype(bf16)
        step(0)

        @pl.loop(0, per_tile)
        def _(k):
            own = pl.ds(pl.multiple_of(t * tile + k * chunk, chunk), chunk)
            i = jnp.where(t < early, 2 * per_tile * t, per_tile * (early + t)) + k
            part[i] = (dot_nt(gg[own, :], wg[...]) + dot_nt(ug[own, :], wu[...])).astype(bf16)
            sums.offer(i)

        step(1)

        @pl.when(t < early)
        def _():
            @pl.loop(0, per_tile)
            def _(k):
                i = 2 * per_tile * t + per_tile + k
                own = pl.ds(pl.multiple_of(k * chunk, chunk), chunk)
                part[i] = dot(inner_s[own, :], wd[...]).astype(bf16)
                sums.offer(i)

        @pl.when(t >= early)
        def _():
            @pl.loop(0, per_tile)
            def _(k):
                own = pl.ds(pl.multiple_of(k * chunk, chunk), chunk)
                late[t - early, own, :] = dot(inner_s[own, :], wd[...]).astype(bf16)

            saving_late(t - early).start()

        step(2)
        step(3)

    begun = (tiles - 1) * per_tile

    @pl.loop(0, count - begun)
    def _(k):
        @pl.when(k < 4)
        def _():
            own = pl.ds(pl.multiple_of(k * tile, tile), tile)
            dwg[own, :] = dot(normed_t[own, :], gg[...]).astype(bf16)

        @pl.when((k >= 4) & (k < 8))
        def _():
            own = pl.ds(pl.multiple_of((k - 4) * tile, tile), tile)
            dwu[own, :] = dot(normed_t[own, :], ug[...]).astype(bf16)

        @pl.when(k >= 8)
        def _():
            share = inner_t.shape[0] // 4
            own = pl.ds(pl.multiple_of((k - 8) * share, 16), share)
            total = jnp.zeros((share, dim), f32)
            for s in range(seqs):
                total = total + dot(inner_t[own, s * rows : (s + 1) * rows], cot[s])
            dwd[own, :] = total.astype(bf16)

        sums.step(begun + k, done)

    sums.close(count, done)

    for t in range(tiles - early):
        saving_late(t).wait()

    @pl.loop(0, count)
    def _(i):
        saving(i).wait()


def feed(tok, attn, cot, g2, wg, wu, wd):
    seqs, rows, dim = tok.shape
    units = wg.shape[1]
    chunk = 64
    tokens = seqs * rows
    count = tokens // chunk * 3 // 2
    vmem = pl.BlockSpec(memory_space=pltpu.VMEM)
    anyw = pl.BlockSpec(memory_space=pl.ANY)
    dma = pltpu.SemaphoreType.DMA
    lines = pltpu.VMEM((count, chunk, dim), bf16)
    tile = 256
    late = tokens // tile // 2
    return pl.pallas_call(
        feed_kernel,
        name="feed",
        out_shape=(
            jax.ShapeDtypeStruct((count, chunk, dim), bf16),
            jax.ShapeDtypeStruct((late, tile, dim), bf16),
            jax.ShapeDtypeStruct((dim, units), bf16),
            jax.ShapeDtypeStruct((dim, units), bf16),
            jax.ShapeDtypeStruct((units, dim), bf16),
        ),
        in_specs=[vmem] * 7,
        out_specs=(anyw, anyw, vmem, vmem, vmem),
        scratch_shapes=[
            pltpu.VMEM((dim, tokens), bf16),
            pltpu.VMEM((units, tokens), bf16),
            pltpu.VMEM((tile, units), bf16),
            pltpu.VMEM((tokens, units), bf16),
            pltpu.VMEM((tokens, units), bf16),
            pltpu.VMEM((late, tile, dim), bf16),
            lines, lines, lines, lines,
            dma((count,)), dma((count,)), dma((count,)), dma((count,)), dma((count,)), dma((late,)),
        ],
        compiler_params=pltpu.CompilerParams(
            collective_id=1, has_side_effects=True, vmem_limit_bytes=60 * 1024 * 1024),
        cost_estimate=pl.CostEstimate(flops=14 * 10**9, bytes_accessed=10**7, transcendentals=10**6),
    )(tok, attn, cot, g2, wg, wu, wd)


def back_kernel(
    tok, attn, cot, mixed, late, g1, g2, wq, wk, wv, wo, q, kv, ctx, lse, cosine, sine, prefix,
    block_hbm, token_hbm, fv_grad, dwq, dwk, dwv, dwo, gains,
    hid, branch, qtm, qm, otm, om, kt, delta, dqt, dk, dv, give, take, proj, normed_t,
    block, part, inward, across, result,
    kv_send, kv_recv, send_one, recv_one, send_two, recv_two, save,
):
    place, ring = lax.axis_index("tp"), lax.axis_index("ctx")
    seqs, rows, dim = tok.shape
    width = wq.shape[1]
    heads = width // HEAD_DIM
    count, chunk = part.shape[0], part.shape[1]
    per_seq = rows // chunk
    mate = {"ctx": ring + 1 - 2 * lax.rem(ring, 2)}
    peer = {"ctx": lax.rem(ring + 2, 4)}
    blocks = (ring, ring + 1 - 2 * lax.rem(ring, 2), lax.rem(ring + 2, 4), 3 - ring)
    greet(place, ring)
    sums = Sum(place, part, inward, across, result, (send_one, recv_one, send_two, recv_two))
    gain_one, gain_two = g1[...].astype(f32), g2[...].astype(f32)
    gains[...] = jnp.zeros_like(gains)

    late_per = late.shape[1] // chunk

    @pl.loop(0, per_seq)
    def _(i):
        own = pl.ds(pl.multiple_of(lax.rem(i, late_per) * chunk, chunk), chunk)
        part[i] = late[i // late_per, own, :]
        sums.offer(i)

    def hidden_at(s, at):
        return tok[s, at, :].astype(f32) + attn[s, at, :].astype(f32)

    def saving_block(i):
        s, own = i // per_seq, pl.ds(pl.multiple_of(lax.rem(i, per_seq) * chunk, chunk), chunk)
        return pltpu.make_async_copy(block.at[i], block_hbm.at[s, own], save.at[i])

    def saving_token(i):
        s, own = i // per_seq, pl.ds(pl.multiple_of(lax.rem(i, per_seq) * chunk, chunk), chunk)
        return pltpu.make_async_copy(hid.at[s, own], token_hbm.at[s, own], save.at[seqs * per_seq + i])

    def done(i):
        @pl.when(i < per_seq)
        def _():
            own = pl.ds(pl.multiple_of(i * chunk, chunk), chunk)
            block[per_seq + i] = (hidden_at(1, own) + result[i].astype(f32)).astype(bf16)
            saving_block(per_seq + i).start()

        @pl.when(i >= per_seq)
        def _():
            n = i - per_seq
            s, own = n // per_seq, pl.ds(pl.multiple_of(lax.rem(n, per_seq) * chunk, chunk), chunk)
            values, upstream = tok[s, own, :].astype(f32), result[i].astype(f32)
            factor = lax.rsqrt(jnp.mean(values * values, axis=-1, keepdims=True) + epsilon)
            scaled = upstream * gain_one
            gains[0:1, :] += jnp.sum(upstream * values * factor, axis=0, keepdims=True)
            hid[s, own, :] += factor * scaled - values * factor**3 * jnp.mean(
                scaled * values, axis=-1, keepdims=True)
            saving_token(n).start()

    def move(s, source, target, device):
        return pltpu.make_async_remote_copy(
            src_ref=give.at[s, source], dst_ref=take.at[s, target], send_sem=kv_send.at[s, source],
            recv_sem=kv_recv.at[s, target], device_id=device, device_id_type=MESH)

    far_to_mate = lambda s: move(s, 2, 0, mate)
    peer_back = lambda s: move(s, 1, 1, peer)
    near_to_mate = lambda s: move(s, 0, 2, mate)
    tile = 256

    for s in range(seqs):
        @pl.loop(0, rows // tile)
        def _(t):
            at = pl.ds(pl.multiple_of(t * tile, tile), tile)
            values = hidden_at(s, at)
            picks = []
            for k in range(tile // chunk):
                n = (s * (rows // tile) + t)
                early = seqs * rows // tile // 2
                per_tile = tile // chunk
                picks.append(mixed[jnp.where(n < early, 2 * per_tile * n, per_tile * (early + n)) + k])
            upstream = jnp.concatenate(picks, axis=0).astype(f32)
            factor = lax.rsqrt(jnp.mean(values * values, axis=-1, keepdims=True) + epsilon)
            scaled = upstream * gain_two
            gains[1:2, :] += jnp.sum(upstream * values * factor, axis=0, keepdims=True)
            hid_now = cot[s, at, :].astype(f32) + factor * scaled - values * factor**3 * jnp.mean(
                scaled * values, axis=-1, keepdims=True)
            hid[s, at, :] = hid_now
            low = hid_now.astype(bf16)
            branch[s, at, :] = low
            grad = dot_nt(low, wo[...])
            lane_owner = lax.broadcasted_iota(jnp.int32, grad.shape, 1) // HEAD_DIM
            q_now = q[s, at, :]
            grad_t = dot_nt(wo[...], low)
            row_owner = lax.broadcasted_iota(jnp.int32, grad_t.shape, 0) // HEAD_DIM
            q_t = jnp.transpose(q_now.astype(f32))
            ctx_t = jnp.transpose(ctx[s, at, :].astype(f32))
            product = grad_t.astype(bf16).astype(f32) * ctx_t
            for h in range(heads):
                om[h, at, :] = jnp.where(lane_owner == h, grad, 0.0).astype(bf16)
                qm[h, at, :] = jnp.where(lane_owner == h, q_now.astype(f32), 0.0).astype(bf16)
                otm[h, :, at] = jnp.where(row_owner == h, grad_t, 0.0).astype(bf16)
                qtm[h, :, at] = jnp.where(row_owner == h, q_t, 0.0).astype(bf16)
                delta[h, :, at] = jnp.sum(
                    product[h * HEAD_DIM : (h + 1) * HEAD_DIM], axis=0, keepdims=True)
            normed = (unit_norm(tok[s, at, :].astype(f32)) * gain_one).astype(bf16)
            flat = pl.ds(pl.multiple_of(s * rows + t * tile, tile), tile)
            normed_t[:, flat] = jnp.transpose(normed)

        dqt[...] = jnp.zeros_like(dqt)

        def back_block(j, block_at, steps):
            kt[...] = jnp.transpose(kv[s, j, 0])
            key_pos = block_at * rows + lax.broadcasted_iota(jnp.int32, (rows, 1), 0)
            query_pos = ring * rows + lax.broadcasted_iota(jnp.int32, (1, rows), 1)
            seen = key_pos < jnp.maximum(query_pos + 1, prefix[s])
            dk[...] = jnp.zeros_like(dk)
            dv[...] = jnp.zeros_like(dv)

            @pl.loop(0, heads)
            def _(h):
                of_head = pl.ds(pl.multiple_of(h * HEAD_DIM, HEAD_DIM), HEAD_DIM)
                scores = dot(kv[s, j, 0], qtm[h])
                probs = jnp.where(seen, jnp.exp(scores - lse[s, pl.ds(h, 1), :]), 0.0)
                dprobs = dot(kv[s, j, 1], otm[h])
                dv[...] += dot(probs.astype(bf16), om[h])
                dscores = (probs * (dprobs - delta[h])).astype(bf16)
                dk[...] += dot(dscores, qm[h])
                dqt[of_head, :] += dot(kt[of_head, :], dscores)

                @pl.when(lax.rem(h, 2) == 1)
                def _():
                    sums.step(steps + h // 2, done)

        base = s * per_seq
        back_block(3, blocks[3], base)
        give[s, 2, 0] = dk[...].astype(bf16)
        give[s, 2, 1] = dv[...].astype(bf16)
        far_to_mate(s).start()
        back_block(2, blocks[2], base + 2)
        far_to_mate(s).wait_recv()
        give[s, 1, 0] = (dk[...] + take[s, 0, 0].astype(f32)).astype(bf16)
        give[s, 1, 1] = (dv[...] + take[s, 0, 1].astype(f32)).astype(bf16)
        peer_back(s).start()
        back_block(1, blocks[1], base + 4)
        give[s, 0, 0] = dk[...].astype(bf16)
        give[s, 0, 1] = dv[...].astype(bf16)
        near_to_mate(s).start()
        back_block(0, blocks[0], base + 6)
        near_to_mate(s).wait_recv()
        peer_back(s).wait_recv()

        @pl.loop(0, rows // tile)
        def _(t):
            at = pl.ds(pl.multiple_of(t * tile, tile), tile)
            flat = pl.ds(pl.multiple_of(s * rows + t * tile, tile), tile)
            co, si = cosine[at, :], sine[at, :]
            grad_v = 0.5 * (dv[at, :] + take[s, 2, 1, at, :].astype(f32) + take[s, 1, 1, at, :].astype(f32))
            fv_grad[s, at, :] = grad_v
            grad_k = dk[at, :] + take[s, 2, 0, at, :].astype(f32) + take[s, 1, 0, at, :].astype(f32)
            grad_q = jnp.transpose(dqt[:, at]) * HEAD_DIM ** (-0.5)
            proj[0, flat, :] = (grad_q * co - turned(grad_q) * si).astype(bf16)
            proj[1, flat, :] = (grad_k * co - turned(grad_k) * si).astype(bf16)
            proj[2, flat, :] = grad_v.astype(bf16)

        @pl.loop(0, per_seq)
        def _(k):
            own = pl.ds(pl.multiple_of(s * rows + k * chunk, chunk), chunk)
            i = per_seq * (s + 1) + k
            part[i] = (
                dot_nt(proj[0, own, :], wq[...]) + dot_nt(proj[1, own, :], wk[...])
                + dot_nt(proj[2, own, :], wv[...])).astype(bf16)
            sums.offer(i)

    @pl.loop(0, 4)
    def _(k):
        own = pl.ds(pl.multiple_of(k * tile, tile), tile)
        dwq[own, :] = dot(normed_t[own, :], proj[0]).astype(bf16)
        dwk[own, :] = dot(normed_t[own, :], proj[1]).astype(bf16)
        dwv[own, :] = dot(normed_t[own, :], proj[2]).astype(bf16)
        sums.step(2 * per_seq + k, done)

    total = jnp.zeros(dwo.shape, f32)
    for s in range(seqs):
        total = total + dot(jnp.transpose(ctx[s]), branch[s])
    dwo[...] = total.astype(bf16)

    @pl.loop(0, per_seq)
    def _(i):
        own = pl.ds(pl.multiple_of(i * chunk, chunk), chunk)
        per_tile = tile // chunk
        at = 2 * per_tile * (i // per_tile) + per_tile + lax.rem(i, per_tile)
        block[i] = (hidden_at(0, own) + mixed[at].astype(f32)).astype(bf16)
        saving_block(i).start()

    @pl.loop(2 * per_seq + 4, count)
    def _(i):
        sums.step(i, done)

    sums.close(count, done)
    for s in range(seqs):
        far_to_mate(s).wait_send()
        peer_back(s).wait_send()
        near_to_mate(s).wait_send()

    @pl.loop(0, seqs * per_seq)
    def _(i):
        saving_block(i).wait()
        saving_token(i).wait()


def back(tok, attn, cot, mixed, late, g1, g2, wq, wk, wv, wo, q, kv, ctx, lse, cosine, sine, prefix):
    seqs, rows, dim = tok.shape
    width = wq.shape[1]
    heads = width // HEAD_DIM
    count, chunk, _ = mixed.shape
    tokens = seqs * rows
    vmem = pl.BlockSpec(memory_space=pltpu.VMEM)
    anyw = pl.BlockSpec(memory_space=pl.ANY)
    dma = pltpu.SemaphoreType.DMA
    lines = pltpu.VMEM((count, chunk, dim), bf16)
    wide = pltpu.VMEM((heads, rows, width), bf16)
    tall = pltpu.VMEM((heads, width, rows), bf16)
    return pl.pallas_call(
        back_kernel,
        name="back",
        out_shape=(
            jax.ShapeDtypeStruct((seqs, rows, dim), bf16),
            jax.ShapeDtypeStruct((seqs, rows, dim), f32),
            jax.ShapeDtypeStruct((seqs, rows, width), f32),
            jax.ShapeDtypeStruct((dim, width), bf16),
            jax.ShapeDtypeStruct((dim, width), bf16),
            jax.ShapeDtypeStruct((dim, width), bf16),
            jax.ShapeDtypeStruct((width, dim), bf16),
            jax.ShapeDtypeStruct((2, dim), f32),
        ),
        in_specs=[vmem] * 17 + [pl.BlockSpec(memory_space=pltpu.SMEM)],
        out_specs=(anyw, anyw) + (vmem,) * 6,
        scratch_shapes=[
            pltpu.VMEM((seqs, rows, dim), f32),
            pltpu.VMEM((seqs, rows, dim), bf16),
            tall, wide, tall, wide,
            pltpu.VMEM((width, rows), bf16),
            pltpu.VMEM((heads, 1, rows), f32),
            pltpu.VMEM((width, rows), f32),
            pltpu.VMEM((rows, width), f32),
            pltpu.VMEM((rows, width), f32),
            pltpu.VMEM((seqs, 3, 2, rows, width), bf16),
            pltpu.VMEM((seqs, 3, 2, rows, width), bf16),
            pltpu.VMEM((3, tokens, width), bf16),
            pltpu.VMEM((dim, tokens), bf16),
            pltpu.VMEM((tokens // chunk, chunk, dim), bf16),
            lines, lines, lines, lines,
            dma((seqs, 3)), dma((seqs, 3)),
            dma((count,)), dma((count,)), dma((count,)), dma((count,)), dma((2 * tokens // chunk,)),
        ],
        compiler_params=pltpu.CompilerParams(
            collective_id=2, has_side_effects=True, vmem_limit_bytes=62 * 1024 * 1024),
        cost_estimate=pl.CostEstimate(flops=30 * 10**9, bytes_accessed=10**7, transcendentals=10**7),
    )(tok, attn, cot, mixed, late, g1, g2, wq, wk, wv, wo, q, kv, ctx, lse, cosine, sine, prefix)


def passed_along(block, axis, distance):
    devices = range(lax.axis_size(axis))
    route = [((i - distance) % len(devices), i) for i in devices]
    return lax.ppermute(block, axis, route)


def rms_scale(values, gain_vector):
    return (
        values
        * lax.rsqrt(jnp.mean(values * values, axis=-1, keepdims=True) + epsilon)
        * gain_vector
    )


def rms_back(values, gain_vector, upstream):
    factor = lax.rsqrt(jnp.mean(values * values, axis=-1, keepdims=True) + epsilon)
    scaled = upstream * gain_vector
    input_grad = factor * scaled - values * factor**3 * jnp.mean(
        scaled * values, axis=-1, keepdims=True
    )
    gain_grad = jnp.sum(upstream * values * factor, axis=(0, 1))
    return (input_grad, gain_grad)


def rope_tables(positions):
    half_dim = HEAD_DIM // 2
    frequency = rope_base ** (-jnp.arange(half_dim, dtype=jnp.float32) / half_dim)
    angles = positions.astype(jnp.float32)[:, None] * frequency[None, :]
    angles = jnp.concatenate([angles, angles], axis=1)
    return (jnp.cos(angles), jnp.sin(angles))


def rotate(values, cosine_table, sine_table):
    half_dim = values.shape[-1] // 2
    turned = jnp.concatenate([-values[..., half_dim:], values[..., :half_dim]], axis=-1)
    return values * cosine_table[:, None, :] + turned * sine_table[:, None, :]


def rotate_back(values, cosine_table, sine_table):
    half_dim = values.shape[-1] // 2
    scaled = values * sine_table[:, None, :]
    turned = jnp.concatenate([scaled[..., half_dim:], -scaled[..., :half_dim]], axis=-1)
    return values * cosine_table[:, None, :] + turned


def contract(left_side, right_side):
    return jnp.einsum("sra,srb->ab", left_side, right_side, preferred_element_type=jnp.float32)


def score_block(query_low, key_low, query_pos, key_pos, limits):
    scores = jnp.einsum(
        "sqhd,skhd->shqk", query_low, key_low, preferred_element_type=jnp.float32
    ) * HEAD_DIM ** (-0.5)
    allowed = (key_pos[None, None, :] <= query_pos[None, :, None]) | (
        key_pos[None, None, :] < limits[:, None, None]
    )
    return (scores, allowed[:, None])


def shards(
    tokens,
    first_values,
    norm1_gain,
    norm2_gain,
    w_query,
    w_key,
    w_value,
    w_out,
    w_gate,
    w_up,
    w_down,
    prefix,
    cotangent,
):
    gathered = (
        lax.all_gather(norm1_gain, "fsdp", axis=0, tiled=True),
        lax.all_gather(norm2_gain, "fsdp", axis=0, tiled=True),
        lax.all_gather(w_query, "fsdp", axis=0, tiled=True),
        lax.all_gather(w_key, "fsdp", axis=0, tiled=True),
        lax.all_gather(w_value, "fsdp", axis=0, tiled=True),
        lax.all_gather(w_out, "fsdp", axis=1, tiled=True),
        lax.all_gather(w_gate, "fsdp", axis=0, tiled=True),
        lax.all_gather(w_up, "fsdp", axis=0, tiled=True),
        lax.all_gather(w_down, "fsdp", axis=1, tiled=True),
    )
    (
        gain_one,
        gain_two,
        full_query,
        full_key,
        full_value,
        full_out,
        full_gate,
        full_up,
        full_down,
    ) = gathered
    seq_count, local_rows = (tokens.shape[0], tokens.shape[1])
    cycle_size = lax.axis_size("ctx")
    my_place = lax.axis_index("ctx")
    local_width = full_query.shape[1]
    head_count = local_width // HEAD_DIM
    shape_four = (seq_count, local_rows, head_count, HEAD_DIM)
    score_scale = HEAD_DIM ** (-0.5)
    positions = my_place * local_rows + jnp.arange(local_rows, dtype=jnp.int32)
    cosine_table, sine_table = rope_tables(positions)
    wide_cos = jnp.tile(cosine_table, (1, head_count))
    half = HEAD_DIM // 2
    signs = jnp.where(jnp.arange(local_width) % HEAD_DIM < half, -1.0, 1.0).astype(f32)
    wide_sin = jnp.tile(sine_table, (1, head_count)) * signs
    attn_sum, query_scaled, pairs, context_low, log_total = attend(
        tokens, first_values, gain_one[None, :], full_query, full_key, full_value, full_out,
        wide_cos, wide_sin, prefix)
    mixed, late, gate_weight_grad, up_weight_grad, down_weight_grad = feed(
        tokens, attn_sum.reshape(tokens.shape), cotangent, gain_two[None, :], full_gate, full_up, full_down)
    (block_out, token_grad, half_value_grad, query_weight_grad, key_weight_grad, value_weight_grad,
     out_weight_grad, gains) = back(
        tokens, attn_sum.reshape(tokens.shape), cotangent, mixed, late, gain_one[None, :], gain_two[None, :],
        full_query, full_key, full_value, full_out, query_scaled, pairs, context_low, log_total,
        wide_cos, wide_sin, prefix)
    gain_one_grad, gain_two_grad = gains[0], gains[1]
    shard_sums = (
        lax.psum_scatter(
            gain_one_grad.astype(jnp.bfloat16), "fsdp", scatter_dimension=0, tiled=True
        ).astype(jnp.float32),
        lax.psum_scatter(
            gain_two_grad.astype(jnp.bfloat16), "fsdp", scatter_dimension=0, tiled=True
        ).astype(jnp.float32),
        lax.psum_scatter(
            query_weight_grad.astype(jnp.bfloat16), "fsdp", scatter_dimension=0, tiled=True
        ).astype(jnp.float32),
        lax.psum_scatter(
            key_weight_grad.astype(jnp.bfloat16), "fsdp", scatter_dimension=0, tiled=True
        ).astype(jnp.float32),
        lax.psum_scatter(
            value_weight_grad.astype(jnp.bfloat16), "fsdp", scatter_dimension=0, tiled=True
        ).astype(jnp.float32),
        lax.psum_scatter(
            out_weight_grad.astype(jnp.bfloat16), "fsdp", scatter_dimension=1, tiled=True
        ).astype(jnp.float32),
        lax.psum_scatter(
            gate_weight_grad.astype(jnp.bfloat16), "fsdp", scatter_dimension=0, tiled=True
        ).astype(jnp.float32),
        lax.psum_scatter(
            up_weight_grad.astype(jnp.bfloat16), "fsdp", scatter_dimension=0, tiled=True
        ).astype(jnp.float32),
        lax.psum_scatter(
            down_weight_grad.astype(jnp.bfloat16), "fsdp", scatter_dimension=1, tiled=True
        ).astype(jnp.float32),
    )
    sum_one, sum_two, sum_query, sum_key, sum_value, sum_out, sum_gate, sum_up, sum_down = (
        shard_sums
    )
    totals = (
        lax.psum(sum_one.astype(jnp.bfloat16), "ctx").astype(jnp.float32),
        lax.psum(sum_two.astype(jnp.bfloat16), "ctx").astype(jnp.float32),
        lax.psum(sum_query.astype(jnp.bfloat16), "ctx").astype(jnp.float32),
        lax.psum(sum_key.astype(jnp.bfloat16), "ctx").astype(jnp.float32),
        lax.psum(sum_value.astype(jnp.bfloat16), "ctx").astype(jnp.float32),
        lax.psum(sum_out.astype(jnp.bfloat16), "ctx").astype(jnp.float32),
        lax.psum(sum_gate.astype(jnp.bfloat16), "ctx").astype(jnp.float32),
        lax.psum(sum_up.astype(jnp.bfloat16), "ctx").astype(jnp.float32),
        lax.psum(sum_down.astype(jnp.bfloat16), "ctx").astype(jnp.float32),
    )
    return (
        block_out,
        token_grad,
        half_value_grad,
        totals[0],
        totals[1],
        totals[2],
        totals[3],
        totals[4],
        totals[5],
        totals[6],
        totals[7],
        totals[8],
    )


def solution(mesh):
    return jax.shard_map(
        shards,
        mesh=mesh,
        in_specs=(
            P("fsdp", "ctx", None),
            P("fsdp", "ctx", "tp"),
            P("fsdp"),
            P("fsdp"),
            P("fsdp", "tp"),
            P("fsdp", "tp"),
            P("fsdp", "tp"),
            P("tp", "fsdp"),
            P("fsdp", "tp"),
            P("fsdp", "tp"),
            P("tp", "fsdp"),
            P("fsdp"),
            P("fsdp", "ctx", None),
        ),
        out_specs=(
            P("fsdp", "ctx", None),
            P("fsdp", "ctx", None),
            P("fsdp", "ctx", "tp"),
            P("fsdp"),
            P("fsdp"),
            P("fsdp", "tp"),
            P("fsdp", "tp"),
            P("fsdp", "tp"),
            P("tp", "fsdp"),
            P("fsdp", "tp"),
            P("fsdp", "tp"),
            P("tp", "fsdp"),
        ),
        check_vma=False,
    )
```

time: 829 us -> 605 us (0.73)
  Pallas kernels: 0 us -> 293 us
  waiting for transfers between devices: 467 us -> 210 us
  matrix products: 147 us -> 0 us
  other arithmetic: 79.4 us -> 8.2 us
  local copies, waits for them, and re-layouts: 49.2 us -> 14.3 us
  blocking collectives: 53.2 us -> 63.2 us
  starting transfers between devices: 9.09 us -> 0.43 us
    pallas_call x0 -> x3, Pallas kernels: none -> 293 us  [the longest x1 109 us: back(): pl.pallas_call(back_kernel, name='back', out_shape=(jax.ShapeDtypeStruct(...]
    psum x4 -> x1, waiting for transfers between devices: 354 us -> 62.3 us  [shards(): lax.psum(sum_gate.astype(jnp.bfloat16), 'ctx').astype(jnp.float32)]
    dot_general x49 -> x0, matrix products: 147 us -> none  [the longest x4 23.7 us: absorb(): jnp.einsum('shqk,skhd->shqd', weights.astype(jnp.bfloat16), key_pair[1],...]
    ppermute x11 -> x0, waiting for transfers between devices: 66 us -> none  [passed_along(): return lax.ppermute(block, axis, route)]
    reduce_scatter x1, waiting for transfers between devices: 0.02 us -> 28.4 us  [shards(): lax.psum_scatter(up_weight_grad.astype(jnp.bfloat16), 'fsdp', scatter_dim...]
    reduce_scatter x1, waiting for transfers between devices: 0.02 us -> 28.3 us  [shards(): lax.psum_scatter(gate_weight_grad.astype(jnp.bfloat16), 'fsdp', scatter_d...]
    convert_element_type x18 -> x1, other arithmetic: 27.4 us -> 0.01 us  [rope_tables(): angles = positions.astype(jnp.float32)[:, None] * frequency[None, :]]
    reduce_scatter x1, waiting for transfers between devices: 0.03 us -> 26.8 us  [shards(): lax.psum_scatter(down_weight_grad.astype(jnp.bfloat16), 'fsdp', scatter_d...]
  transfers between devices with their start and end apart: 25 -> 11, of which waited for: 15 -> 8; matrix products, arithmetic and copies ran while one was open for 23% -> 1% of each run, Pallas kernels for 0% -> 14%
where the time goes in v1:
time: 605 us; the launch traced here: 604 us
  Pallas kernels  293 us (48%)
  waiting for transfers between devices  210 us (35%)
  blocking collectives  63.2 us (10%)
  between operations  14.8 us (2%)
  local copies, waits for them, and re-layouts  14.3 us (2%)
  other arithmetic  8.2 us (1%)
    pallas_call x1, Pallas kernels, back(): pl.pallas_call(back_kernel, name='back', out_shape=(jax.ShapeDtypeStruct(...  109 us
    pallas_call x1, Pallas kernels, feed(): pl.pallas_call(feed_kernel, name='feed', out_shape=(jax.ShapeDtypeStruct(...  97.7 us
    pallas_call x1, Pallas kernels, attend(): pl.pallas_call(attend_kernel, name='attend', out_shape=(jax.ShapeDtypeStr...  86.4 us
    psum x1, waiting for transfers between devices, shards(): lax.psum(sum_gate.astype(jnp.bfloat16), 'ctx').astype(jnp.float32)  62.3 us
    reduce_scatter x1, waiting for transfers between devices, shards(): lax.psum_scatter(up_weight_grad.astype(jnp.bfloat16), 'fsdp', scatter_dim...  28.4 us
    reduce_scatter x1, waiting for transfers between devices, shards(): lax.psum_scatter(gate_weight_grad.astype(jnp.bfloat16), 'fsdp', scatter_d...  28.3 us
    reduce_scatter x1, waiting for transfers between devices, shards(): lax.psum_scatter(down_weight_grad.astype(jnp.bfloat16), 'fsdp', scatter_d...  26.8 us
    reduce_scatter x1, waiting for transfers between devices, shards(): lax.psum_scatter(query_weight_grad.astype(jnp.bfloat16), 'fsdp', scatter_...  16.9 us
  transfers between devices with their start and end apart: 11, of which 8 were waited for; matrix products, arithmetic and copies ran while one was open for 1% of the time, Pallas kernels for 14%

profile of v1, /device:TPU:0, one launch (start us, length us, event | category | flops | bytes accessed | tf_op | source)
XLA Modules:
  0.0 604.4 jit_solution(14018817392269208185)
XLA Ops:
  7.2 2.3 copy.38
  9.6 1.2 copy.39
  12.0 10.3 %all_gather.28.wq = bf16[1024,256]{1,0:T(8,128)(2,1)} all-gather(bf16[512,256]{1,0:T(8,128)(2,1)S(1)} %copy-done.6), channel_id=1, replica_groups=mesh['fsdp'=2,'ctx'=4,'tp'=4] {'fsdp'}, dimensions={0}, use_global_device_ids=true | all-gather | bytes 786432 | tf_op jit(solution)/shard_map/all_gather | solution.py:787
  22.6 1.0 copy.37.cosine
  23.6 4.9 all-gather
  28.5 4.5 all-gather.1
  33.1 12.6 %all_gather.29.wk = bf16[1024,256]{1,0:T(8,128)(2,1)} all-gather(bf16[512,256]{1,0:T(8,128)(2,1)S(1)} %copy-done.7), channel_id=1, replica_groups=mesh['fsdp'=2,'ctx'=4,'tp'=4] {'fsdp'}, dimensions={0}, use_global_device_ids=true | all-gather | bytes 786432 | tf_op jit(solution)/shard_map/all_gather | solution.py:788
  45.6 7.4 %all_gather.30.wv = bf16[1024,256]{1,0:T(8,128)(2,1)} all-gather(bf16[512,256]{1,0:T(8,128)(2,1)S(1)} %copy-done.8), channel_id=1, replica_groups=mesh['fsdp'=2,'ctx'=4,'tp'=4] {'fsdp'}, dimensions={0}, use_global_device_ids=true | all-gather | bytes 786432 | tf_op jit(solution)/shard_map/all_gather | solution.py:789
  53.0 12.6 %all_gather.31.wo = bf16[256,1024]{1,0:T(8,128)(2,1)} all-gather(bf16[256,512]{1,0:T(8,128)(2,1)S(1)} %copy-done.9), channel_id=1, replica_groups=mesh['fsdp'=2,'ctx'=4,'tp'=4] {'fsdp'}, dimensions={1}, use_global_device_ids=true | all-gather | bytes 786432 | tf_op jit(solution)/shard_map/all_gather | solution.py:790
  65.6 0.8 broadcast_multiply_fusion.sine
  66.4 86.4 %attend.1 = (bf16[16,64,1024]{2,1,0:T(8,128)(2,1)}, bf16[2,512,256]{2,1,0:T(8,128)(2,1)}, bf16[2,4,2,512,256]{4,3,2,1,0:T(8,128)(2,1)}, bf16[2,512,256]{2,1,0:T(8,128)(2,1)}, f32[2,4,512]{2,1,0:T(4,128)}) custom-call(bf16[2,512,1024]{2,1,0:T(8,128)(2,1)} %tok.5, bf16[2,512,256]{2,1,0:T(8,128)(2,1)} %fv.1, bf16[1,1024]{1,0:T(2,128)(2,1)} %bitcast.8, ...), custom_call_target="tpu_custom_call" | custom-call | flops 8000000000 | bytes 10000000 | tf_op jit(solution)/shard_map/attend/pallas_call | solution.py:257
  152.9 97.7 %feed.1 = (bf16[24,64,1024]{2,1,0:T(8,128)(2,1)}, bf16[2,256,1024]{2,1,0:T(8,128)(2,1)}, bf16[1024,704]{1,0:T(8,128)(2,1)}, bf16[1024,704]{1,0:T(8,128)(2,1)}, bf16[704,1024]{1,0:T(8,128)(2,1)}) custom-call(bf16[2,512,1024]{2,1,0:T(8,128)(2,1)} %tok.5, bf16[2,512,1024]{2,1,0:T(8,128)(2,1)} %bitcast.12, bf16[2,512,1024]{2,1,0:T(8,128)(2,1)} %cot.3, ...), custom_call_target="tpu_custom_call" | custom-call | flops 14000000000 | bytes 10000000 | tf_op jit(solution)/shard_map/feed/pallas_call | solution.py:421
  250.6 109.3 %back.1 = (bf16[2,512,1024]{2,1,0:T(8,128)(2,1)}, f32[2,512,1024]{2,1,0:T(8,128)}, f32[2,512,256]{2,1,0:T(8,128)}, bf16[1024,256]{1,0:T(8,128)(2,1)}, bf16[1024,...) custom-call(bf16[2,512,1024]{2,1,0:T(8,128)(2,1)} %tok.5, ...), custom_call_target="tpu_custom_call" | custom-call | flops 30000001024 | bytes 10000000 | tf_op jit(solution)/shard_map/back/pallas_call | solution.py:671
  364.0 9.5 %reduce-scatter.10.cloned.1.call-done = bf16[512,256]{1,0:T(8,128)(2,1)} async-done(((bf16[1024,256]{1,0:T(8,128)(2,1)}), bf16[512,256]{1,0:T(8,128)(2,1)}) %reduce-scatter.10.cloned.1.call-update) | async-done | bytes 262160 | tf_op jit(solution)/shard_map/reduce_scatter | solution.py:840
  373.4 16.8 %reduce-scatter.12.cloned.1.call-done = bf16[512,256]{1,0:T(8,128)(2,1)} async-done(((bf16[1024,256]{1,0:T(8,128)(2,1)}), bf16[512,256]{1,0:T(8,128)(2,1)}) %reduce-scatter.12.cloned.1.call-update) | async-done | bytes 262160 | tf_op jit(solution)/shard_map/reduce_scatter | solution.py:843
  390.2 16.7 %reduce-scatter.14.cloned.1.call-done = bf16[256,512]{1,0:T(8,128)(2,1)} async-done(((bf16[256,1024]{1,0:T(8,128)(2,1)}), bf16[256,512]{1,0:T(8,128)(2,1)}) %reduce-scatter.14.cloned.1.call-update) | async-done | bytes 262160 | tf_op jit(solution)/shard_map/reduce_scatter | solution.py:846
  406.9 16.9 %reduce-scatter.8.cloned.1.call-done = bf16[512,256]{1,0:T(8,128)(2,1)} async-done(((bf16[1024,256]{1,0:T(8,128)(2,1)}), bf16[512,256]{1,0:T(8,128)(2,1)}) %reduce-scatter.8.cloned.1.call-update) | async-done | bytes 262160 | tf_op jit(solution)/shard_map/reduce_scatter | solution.py:837
  423.8 28.3 %reduce-scatter.16.cloned.1.call-done = bf16[512,704]{1,0:T(8,128)(2,1)} async-done(((bf16[1024,704]{1,0:T(8,128)(2,1)}), bf16[512,704]{1,0:T(8,128)(2,1)}) %reduce-scatter.16.cloned.1.call-update) | async-done | bytes 720912 | tf_op jit(solution)/shard_map/reduce_scatter | solution.py:849
  452.1 28.4 %reduce-scatter.18.cloned.1.call-done = bf16[512,704]{1,0:T(8,128)(2,1)} async-done(((bf16[1024,704]{1,0:T(8,128)(2,1)}), bf16[512,704]{1,0:T(8,128)(2,1)}) %reduce-scatter.18.cloned.1.call-update) | async-done | bytes 720912 | tf_op jit(solution)/shard_map/reduce_scatter | solution.py:852
  480.6 26.8 %reduce-scatter.20.cloned.1.call-done = bf16[704,512]{1,0:T(8,128)(2,1)} async-done(((bf16[704,1024]{1,0:T(8,128)(2,1)}), bf16[704,512]{1,0:T(8,128)(2,1)}) %reduce-scatter.20.cloned.1.call-update) | async-done | bytes 720912 | tf_op jit(solution)/shard_map/reduce_scatter | solution.py:855
  508.7 4.9 all-reduce.4
  513.8 6.0 %all-reduce.2 = (bf16[512]{0:T(512)(128)(2,1)S(1)}, bf16[512]{0:T(512)(128)(2,1)S(1)}) all-reduce(bf16[512]{0:T(512)(128)(2,1)S(1)} %dynamic-slice.1, bf16[512]{0:T(512)(128)(2,1)S(1)} %dynamic-slice.3), channel_id=1, replica_groups=mesh['fsdp'=2,'ctx'=4,'tp'=4] {'ctx'}, use_global_device_ids=true, to_apply=%region_1.2 | all-reduce | flops 1024 | bytes 4096 | tf_op jit(solution)/shard_map/psum | solution.py:863
  521.0 62.3 %all-reduce.7.cloned.1.call-done = (bf16[512,704]{1,0:T(8,128)(2,1)}, bf16[512,704]{1,0:T(8,128)(2,1)}, bf16[512,256]{1,0:T(8,128)(2,1)}, bf16[512,256]{1,0:T(8,...) async-done(((bf16[512,704]{1,0:T(8,128)(2,1)}, bf16[512,704]{1,0:T(8,128)(2,1)}, bf16[512,256]{1,0:T(8,128)(2,1)}, ...) | async-done | bytes 3211280 | tf_op jit(solution)/shard_map/psum | solution.py:869
  583.4 2.5 convert_element_type.71
  585.9 1.4 copy.41
  587.3 1.4 copy.42
  588.6 0.8 convert_element_type.65
  591.1 0.9 convert_element_type.68
  592.0 1.3 copy.53
  593.3 1.6 copy-done
  594.9 2.0 copy.54
  596.9 1.0 copy.55
  (79 shorter events, 9.2 us)
Async XLA Ops:
  7.2 2.5 copy-start.5
  7.2 145.7 %all-gather.6.cloned.1.call-start = ((), (), s32[]{:S(2)}) async-start(), calls=%async_computation.7 | async-start | bytes 2359296 | tf_op jit(solution)/shard_map/all_gather | solution.py:791
  9.6 2.4 copy-start.6
  9.6 143.3 %all-gather.8.cloned.1.call-start = ((), (), s32[]{:S(2)}) async-start(), calls=%async_computation.8 | async-start | bytes 2359296 | tf_op jit(solution)/shard_map/all_gather | solution.py:792
  10.8 142.1 %all-gather.10.cloned.1.call-start = ((), (), s32[]{:S(2)}) async-start(), calls=%async_computation.9 | async-start | bytes 2162688 | tf_op jit(solution)/shard_map/all_gather | solution.py:793
  11.6 361.9 %reduce-scatter.10.cloned.1.call-start = ((), (), s32[]{:S(2)}) async-start(), calls=%async_computation.11 | async-start | bytes 786432 | tf_op jit(solution)/shard_map/reduce_scatter | solution.py:840
  12.0 11.7 %copy-start.15 = (bf16[512]{0:T(512)(128)(2,1)S(1)}, bf16[512]{0:T(512)(128)(2,1)}, u32[]{:S(2)}) copy-start(bf16[512]{0:T(512)(128)(2,1)} %param.15) | copy-start | bytes 3076
  12.0 11.6 %copy-start.16 = (bf16[512]{0:T(512)(128)(2,1)S(1)}, bf16[512]{0:T(512)(128)(2,1)}, u32[]{:S(2)}) copy-start(bf16[512]{0:T(512)(128)(2,1)} %param.16) | copy-start | bytes 3076
  12.0 21.1 %copy-start.7 = (bf16[512,256]{1,0:T(8,128)(2,1)S(1)}, bf16[512,256]{1,0:T(8,128)(2,1)}, u32[]{:S(2)}) copy-start(bf16[512,256]{1,0:T(8,128)(2,1)} %param.18) | copy-start | bytes 786436
  22.3 23.4 %copy-start.8 = (bf16[512,256]{1,0:T(8,128)(2,1)S(1)}, bf16[512,256]{1,0:T(8,128)(2,1)}, u32[]{:S(2)}) copy-start(bf16[512,256]{1,0:T(8,128)(2,1)} %param.19) | copy-start | bytes 786436
  22.3 30.7 %copy-start.9 = (bf16[256,512]{1,0:T(8,128)(2,1)S(1)}, bf16[256,512]{1,0:T(8,128)(2,1)}, u32[]{:S(2)}) copy-start(bf16[256,512]{1,0:T(8,128)(2,1)} %param.20) | copy-start | bytes 786436
  359.9 30.3 %reduce-scatter.12.cloned.1.call-start = ((), (), s32[]{:S(2)}) async-start(), calls=%async_computation.12 | async-start | bytes 786432 | tf_op jit(solution)/shard_map/reduce_scatter | solution.py:843
  360.5 46.3 %reduce-scatter.14.cloned.1.call-start = ((), (), s32[]{:S(2)}) async-start(), calls=%async_computation.13 | async-start | bytes 786432 | tf_op jit(solution)/shard_map/reduce_scatter | solution.py:846
  361.1 62.7 %reduce-scatter.8.cloned.1.call-start = ((), (), s32[]{:S(2)}) async-start(), calls=%async_computation.10 | async-start | bytes 786432 | tf_op jit(solution)/shard_map/reduce_scatter | solution.py:837
  361.9 90.3 %reduce-scatter.16.cloned.1.call-start = ((), (), s32[]{:S(2)}) async-start(), calls=%async_computation.14 | async-start | bytes 2359296 | tf_op jit(solution)/shard_map/reduce_scatter | solution.py:849
  362.6 118.0 %reduce-scatter.18.cloned.1.call-start = ((), (), s32[]{:S(2)}) async-start(), calls=%async_computation.15 | async-start | bytes 2359296 | tf_op jit(solution)/shard_map/reduce_scatter | solution.py:852
  363.3 144.0 %reduce-scatter.20.cloned.1.call-start = ((), (), s32[]{:S(2)}) async-start(), calls=%async_computation.16 | async-start | bytes 2162688 | tf_op jit(solution)/shard_map/reduce_scatter | solution.py:855
  363.4 144.0 %copy-start.17 = (u32[32]{0:T(128)S(1)}, u32[32]{0:T(128)}, u32[]{:S(2)}) copy-start(u32[32]{0:T(128)} %constant.36) | copy-start | bytes 388
  363.4 145.2 %copy-start.14 = (f32[2,1024]{1,0:T(2,128)S(1)}, f32[2,1024]{1,0:T(2,128)}, u32[]{:S(2)}) copy-start(f32[2,1024]{1,0:T(2,128)} %get-tuple-element.40) | copy-start | bytes 24580
  363.9 219.4 %all-reduce.7.cloned.1.call-start = ((), (), s32[]{:S(2)}) async-start(), calls=%async_computation.17 | async-start | bytes 6684672 | tf_op jit(solution)/shard_map/psum | solution.py:869
  583.4 2.5 copy-start.4
  583.4 3.9 copy-start.3
  585.9 2.7 copy-start.13
  585.9 3.6 copy-start.12
  587.3 3.0 copy-start.11
  587.3 3.9 copy-start.10
  588.6 3.4 copy-start.1
  592.0 2.9 copy-start
  594.9 2.0 copy-start.2
Sparse Core Ops, SparseCore 0:
  10.1 34.9 all-gather.5
  47.2 29.8 all-gather.7
  78.7 25.8 all-gather.9
  360.1 13.3 reduce-scatter.9
  375.6 14.5 reduce-scatter.11
  392.3 14.5 reduce-scatter.13
  409.2 14.5 reduce-scatter.7
  426.1 26.0 reduce-scatter.15
  454.5 26.0 reduce-scatter.17
  482.7 24.6 reduce-scatter.19
  510.5 72.8 all-reduce.6

commit v2 on v1

v2 whole, which is shorter than its diff:
```python
import functools

import jax
import jax.numpy as jnp
from jax import lax
from jax.experimental import pallas as pl
from jax.experimental.pallas import tpu as pltpu
from jax.sharding import PartitionSpec as P

HEAD_DIM = 64
epsilon = 1e-06
rope_base = 10000.0
masked_score = -1e30
MESH = pl.DeviceIdType.MESH
bf16 = jnp.bfloat16
f32 = jnp.float32


def dot(a, b):
    return jnp.dot(a, b, preferred_element_type=f32)


def dot_nt(a, b):
    return lax.dot_general(a, b, (((1,), (1,)), ((), ())), preferred_element_type=f32)


def unit_norm(values):
    return values * lax.rsqrt(jnp.mean(values * values, axis=-1, keepdims=True) + epsilon)


def low_half(shape):
    return lax.rem(lax.broadcasted_iota(jnp.int32, shape, 1), HEAD_DIM) < HEAD_DIM // 2


def turned(values):
    pieces = []
    half = HEAD_DIM // 2
    for at in range(0, values.shape[1], 128):
        piece = values[:, at : at + 128]
        up = pltpu.roll(piece, 128 - half, 1)
        down = pltpu.roll(piece, half, 1)
        pieces.append(jnp.where(low_half(piece.shape), up, down))
    return jnp.concatenate(pieces, axis=1)


class Sum:
    def __init__(self, place, part, inward, across, result, sems):
        self.pair = place + 1 - 2 * lax.rem(place, 2)
        self.middle = 3 - place
        self.inner = (place == 1) | (place == 2)
        self.outer = (place == 0) | (place == 3)
        self.part, self.inward, self.across, self.result = part, inward, across, result
        self.send_one, self.recv_one, self.send_two, self.recv_two = sems

    def copy_in(self, i):
        return pltpu.make_async_remote_copy(
            src_ref=self.part.at[i], dst_ref=self.inward.at[i], send_sem=self.send_one.at[i],
            recv_sem=self.recv_one.at[i], device_id={"tp": self.pair}, device_id_type=MESH)

    def copy_across(self, i):
        return pltpu.make_async_remote_copy(
            src_ref=self.part.at[i], dst_ref=self.across.at[i], send_sem=self.send_two.at[i],
            recv_sem=self.recv_two.at[i], device_id={"tp": self.middle}, device_id_type=MESH)

    def copy_out(self, i):
        return pltpu.make_async_remote_copy(
            src_ref=self.result.at[i], dst_ref=self.result.at[i], send_sem=self.send_one.at[i],
            recv_sem=self.recv_one.at[i], device_id={"tp": self.pair}, device_id_type=MESH)

    def offer(self, i):
        @pl.when(self.outer)
        def _():
            self.copy_in(i).start()

    def take_in(self, i):
        self.copy_in(i).wait_recv()
        self.part[i] = (self.part[i].astype(f32) + self.inward[i].astype(f32)).astype(bf16)
        self.copy_across(i).start()

    def finish(self, i):
        self.copy_across(i).wait_recv()
        self.result[i] = (self.part[i].astype(f32) + self.across[i].astype(f32)).astype(bf16)
        self.copy_out(i).start()

    def step(self, i, done):
        @pl.when(self.inner)
        def _():
            self.take_in(i)

            @pl.when(i > 0)
            def _():
                self.finish(i - 1)
                done(i - 1)

    def close(self, count, done):
        @pl.when(self.inner)
        def _():
            self.finish(count - 1)
            done(count - 1)

            @pl.loop(0, count)
            def _(i):
                self.copy_across(i).wait_send()
                self.copy_out(i).wait_send()

        @pl.when(self.outer)
        def _():
            @pl.loop(0, count)
            def _(i):
                self.copy_out(i).wait_recv()
                done(i)

            @pl.loop(0, count)
            def _(i):
                self.copy_in(i).wait_send()


def near(place):
    return place + 1 - 2 * lax.rem(place, 2)


def greet(peers):
    barrier = pltpu.get_barrier_semaphore()
    for peer in peers:
        pl.semaphore_signal(barrier, inc=1, device_id=peer, device_id_type=MESH)
    pl.semaphore_wait(barrier, len(peers))


def line_peers(place):
    return [{"tp": near(place)}, {"tp": 3 - place}]


def ring_peers(ring):
    return [{"ctx": near(ring)}, {"ctx": lax.rem(ring + 2, 4)}]


def remote(source, target, send, recv, device):
    return pltpu.make_async_remote_copy(
        src_ref=source, dst_ref=target, send_sem=send, recv_sem=recv,
        device_id=device, device_id_type=MESH)


def rows_at(start, size):
    return pl.ds(pl.multiple_of(start, size), size)


class Fold:
    def __init__(self, side, ring, grad, refs, sems, saved):
        self.side, self.half = side, lax.rem(ring, 2)
        self.grad = grad
        self.one, self.two, self.three, self.final = refs
        self.send, self.recv, self.save = sems
        self.mate, self.peer, self.other = (
            {"ctx": near(ring)}, {"ctx": lax.rem(ring + 2, 4)}, {"fsdp": 1 - side})
        self.saved = saved

    def copy(self, n):
        source, target, device = (
            (self.grad.at[1 - self.half], self.one, self.mate),
            (self.grad.at[self.half, 1 - self.side], self.two, self.other),
            (self.grad.at[self.half, self.side], self.three, self.peer),
            (self.final.at[self.half], self.final.at[self.half], self.mate),
        )[n]
        return remote(source, target, self.send.at[n], self.recv.at[n], device)

    def first(self):
        self.copy(0).start()

    def second(self):
        self.copy(0).wait_recv()
        for side in range(2):
            self.grad[self.half, side] = (
                self.grad[self.half, side].astype(f32) + self.one[side].astype(f32)).astype(bf16)
        self.copy(1).start()

    def third(self):
        self.copy(1).wait_recv()
        self.grad[self.half, self.side] = (
            self.grad[self.half, self.side].astype(f32) + self.two[...].astype(f32)).astype(bf16)
        self.copy(2).start()

    def fourth(self):
        self.copy(2).wait_recv()
        self.final[self.half] = (
            self.grad[self.half, self.side].astype(f32) + self.three[...].astype(f32)).astype(bf16)
        self.copy(3).start()

    def saving(self):
        return pltpu.make_async_copy(self.final, self.saved, self.save)

    def last(self):
        self.copy(3).wait_recv()
        self.saving().start()

    def settle(self):
        for n in range(4):
            self.copy(n).wait_send()
        self.saving().wait()


class Whole:
    def __init__(self, grad, sems, saved):
        self.copy = lambda: pltpu.make_async_copy(grad, saved, sems[2])

    def first(self):
        self.copy().start()

    def second(self):
        pass

    third = fourth = last = second

    def settle(self):
        self.copy().wait()


def fold_shapes(shapes, split):
    scratch = []
    for r, c in shapes:
        scratch.append(pltpu.VMEM((2, 2, r, c), bf16))
        if split:
            scratch += [pltpu.VMEM((2, r, c), bf16), pltpu.VMEM((r, c), bf16), pltpu.VMEM((r, c), bf16),
                        pltpu.VMEM((2, r, c), bf16)]
    n = len(shapes)
    dma = pltpu.SemaphoreType.DMA
    scratch += [dma((n, 4)), dma((n, 4)), dma((n,))]
    outs = [jax.ShapeDtypeStruct((2, r, c) if split else (2, 2, r, c), bf16) for r, c in shapes]
    return scratch, outs


def make_folds(split, side, ring, scratch, saved):
    send, recv, save = scratch[-3:]
    folds, grads = [], []
    per = 5 if split else 1
    for n, target in enumerate(saved):
        mine = scratch[n * per : (n + 1) * per]
        sems = (send.at[n], recv.at[n], save.at[n])
        grads.append(mine[0])
        folds.append(
            Fold(side, ring, mine[0], mine[1:], sems, target) if split else Whole(mine[0], sems, target))
    return folds, grads


def gain_row(gains, which):
    return jnp.concatenate([gains[0, which : which + 1, :], gains[1, which : which + 1, :]], axis=1)


def attend_kernel(split, *refs):
    place, ring, side = lax.axis_index("tp"), lax.axis_index("ctx"), lax.axis_index("fsdp")
    (tok, fv, g1, g2, wq_in, wk_in, wv_in, wo_in), refs = refs[:8], refs[8:]
    if split:
        (wg_in, wu_in, wd_in), refs = refs[:3], refs[3:]
    (cosine, sine, prefix, sum_hbm, q_out, kv_hbm, ctx_out, lse_out, gains), refs = refs[:9], refs[9:]
    if split:
        (wq_hbm, wk_hbm, wv_hbm, wo_hbm, wg_out, wu_out, wd_out), refs = refs[:7], refs[7:]
        (wq, wk, wv, wo, w_send, w_recv, w_save, g_sems), refs = refs[:8], refs[8:]
    else:
        wq, wk, wv, wo = wq_in, wk_in, wv_in, wo_in
    (normed_s, kv, qtm, vt, acct, maxes, totals, part, inward, across, result,
     kv_send, kv_recv, kv_save, send_one, recv_one, send_two, recv_two, save) = refs
    seqs, rows, width = q_out.shape
    heads = width // HEAD_DIM
    tile = 256
    per_seq = part.shape[0] // seqs
    chunk = part.shape[1]
    mate, peer = ring_peers(ring)
    half = lax.rem(ring, 2)
    blocks = (ring, near(ring), lax.rem(ring + 2, 4), 3 - ring)
    greet(line_peers(place) + ring_peers(ring) + ([{"fsdp": 1 - side}] if split else []))

    if split:
        other = {"fsdp": 1 - side}
        gains[side, 0:1, :] = g1[...].astype(f32)
        gains[side, 1:2, :] = g2[...].astype(f32)
        move_gains = remote(gains.at[side], gains.at[side], g_sems.at[0], g_sems.at[1], other)
        move_gains.start()

        def spot(full, owner, part_at, size):
            if full.shape[0] == 2:
                return full.at[owner, rows_at(part_at * size, size)]
            return full.at[rows_at((2 * owner + part_at) * size, size)]

        def outside(full, owner, part_at, size):
            return full.at[rows_at(part_at * size, size)]

        table = (
            (wk_in, wk, spot), (wv_in, wv, spot), (wq_in, wq, spot), (wo_in, wo, spot),
            (wg_in, wg_out, outside), (wu_in, wu_out, outside), (wd_in, wd_out, outside))

        def cross(n):
            own, full, where = table[n]
            size = own.shape[0] // 2
            return remote(own.at[rows_at(half * size, size)], where(full, side, half, size),
                          w_send.at[n, 0], w_recv.at[n, 0], other)

        def onto_mate(n):
            own, full, where = table[n]
            here = where(full, 1 - side, half, own.shape[0] // 2)
            return remote(here, here, w_send.at[n, 1], w_recv.at[n, 1], mate)

        def hand_on(n):
            cross(n).wait_recv()
            onto_mate(n).start()

        saves = tuple(
            pltpu.make_async_copy(full, target, w_save.at[n])
            for n, (full, target) in enumerate(((wk, wk_hbm), (wv, wv_hbm), (wq, wq_hbm), (wo, wo_hbm))))
        for n in range(7):
            cross(n).start()
        for own, full, _ in table[:3]:
            full[rows_at(side * own.shape[0], own.shape[0]), :] = own[...]
        wo[side] = wo_in[...]
        remote(gains.at[side], gains.at[side], g_sems.at[0], g_sems.at[1], other).wait()
    else:
        for n, gain in enumerate((g1, g2)):
            size = gain.shape[1] // 2
            for piece in range(2):
                gains[piece, n : n + 1, :] = gain[:, piece * size : (piece + 1) * size].astype(f32)

    def pass_block(s, source, target, device, slot):
        return remote(kv.at[s, source], kv.at[s, target], kv_send.at[s, slot], kv_recv.at[s, target], device)

    to_mate = lambda s: pass_block(s, 0, 1, mate, 0)
    to_peer = lambda s: pass_block(s, 0, 2, peer, 1)
    onward = lambda s: pass_block(s, 2, 3, mate, 2)
    gain_one = gain_row(gains, 0)

    for s in range(seqs):
        @pl.loop(0, rows // tile)
        def _(t):
            at = rows_at(t * tile, tile)
            normed_s[s, at, :] = (unit_norm(tok[s, at, :].astype(f32)) * gain_one).astype(bf16)

    if split:
        hand_on(0)
        hand_on(1)
        onto_mate(0).wait_recv()
        onto_mate(1).wait_recv()

    for s in range(seqs):
        @pl.loop(0, rows // tile)
        def _(t):
            at = rows_at(t * tile, tile)
            normed = normed_s[s, at, :]
            co, si = cosine[at, :], sine[at, :]
            k = dot(normed, wk[...])
            kv[s, 0, 0, at, :] = (k * co + turned(k) * si).astype(bf16)
            v = dot(normed, wv[...])
            kv[s, 0, 1, at, :] = (0.5 * v + 0.5 * fv[s, at, :].astype(f32)).astype(bf16)

        to_peer(s).start()
        to_mate(s).start()

    if split:
        hand_on(2)
        hand_on(3)
        onto_mate(2).wait_recv()

    for s in range(seqs):
        @pl.loop(0, rows // tile)
        def _(t):
            at = rows_at(t * tile, tile)
            q = dot(normed_s[s, at, :], wq[...])
            q = (q * cosine[at, :] + turned(q) * sine[at, :]) * HEAD_DIM ** (-0.5)
            q_out[s, at, :] = q.astype(bf16)
            qt = jnp.transpose(q)
            owner = lax.broadcasted_iota(jnp.int32, qt.shape, 0) // HEAD_DIM
            for h in range(heads):
                qtm[s, h, :, at] = jnp.where(owner == h, qt, 0.0).astype(bf16)

    def saving(i):
        return pltpu.make_async_copy(result.at[i], sum_hbm.at[i], save.at[i])

    done = lambda i: saving(i).start()
    sums = Sum(place, part, inward, across, result, (send_one, recv_one, send_two, recv_two))

    def attend_block(s, j, block, steps):
        vt[...] = jnp.transpose(kv[s, j, 1])
        key_pos = block * rows + lax.broadcasted_iota(jnp.int32, (rows, 1), 0)
        query_pos = ring * rows + lax.broadcasted_iota(jnp.int32, (1, rows), 1)
        seen = key_pos < jnp.maximum(query_pos + 1, prefix[s])

        @pl.loop(0, heads)
        def _(h):
            of_head = rows_at(h * HEAD_DIM, HEAD_DIM)
            scores = jnp.where(seen, dot(kv[s, j, 0], qtm[s, h]), masked_score)
            old = maxes[h]
            new = jnp.maximum(old, jnp.max(scores, axis=0, keepdims=True))
            weights = jnp.exp(scores - new)
            fade = jnp.exp(old - new)
            maxes[h] = new
            totals[h] = totals[h] * fade + jnp.sum(weights, axis=0, keepdims=True)
            acct[of_head, :] = acct[of_head, :] * fade + dot(vt[of_head, :], weights.astype(bf16))
            if steps is not None:
                @pl.when(lax.rem(h, 2) == 1)
                def _():
                    sums.step(steps + h // 2, done)

    for s in range(seqs):
        maxes[...] = jnp.full_like(maxes, masked_score)
        totals[...] = jnp.zeros_like(totals)
        acct[...] = jnp.zeros_like(acct)
        begun = lambda j: None if s == 0 else (s - 1) * per_seq + 2 * j
        attend_block(s, 0, blocks[0], begun(0))
        to_mate(s).wait_recv()
        attend_block(s, 1, blocks[1], begun(1))
        to_peer(s).wait_recv()
        onward(s).start()
        attend_block(s, 2, blocks[2], begun(2))
        onward(s).wait_recv()
        attend_block(s, 3, blocks[3], begun(3))
        pltpu.make_async_copy(kv.at[s], kv_hbm.at[s], kv_save.at[s]).start()
        for h in range(heads):
            lse_out[s, h : h + 1, :] = maxes[h] + jnp.log(totals[h])
            of_head = slice(h * HEAD_DIM, (h + 1) * HEAD_DIM)
            acct[of_head, :] = acct[of_head, :] / totals[h]
        ctx_out[s] = jnp.transpose(acct[...]).astype(bf16)
        if split and s == 0:
            onto_mate(3).wait_recv()
            for copy in saves:
                copy.start()

        @pl.loop(0, per_seq)
        def _(i):
            at = rows_at(i * chunk, chunk)
            n = s * per_seq + i
            size = wo.shape[2]
            for piece in range(2):
                part[n, :, piece * size : (piece + 1) * size] = dot(ctx_out[s, at, :], wo[piece]).astype(bf16)
            sums.offer(n)

        if split and s == 0:
            hand_on(4)
            hand_on(5)
        if split and s == seqs - 1:
            hand_on(6)

    @pl.loop((seqs - 1) * per_seq, seqs * per_seq)
    def _(i):
        sums.step(i, done)

    sums.close(seqs * per_seq, done)
    for s in range(seqs):
        to_mate(s).wait_send()
        to_peer(s).wait_send()
        onward(s).wait_send()
        pltpu.make_async_copy(kv.at[s], kv_hbm.at[s], kv_save.at[s]).wait()

    @pl.loop(0, seqs * per_seq)
    def _(i):
        saving(i).wait()

    if split:
        for n in range(4, 7):
            onto_mate(n).wait_recv()
        for n in range(7):
            cross(n).wait_send()
            onto_mate(n).wait_send()
        for copy in saves:
            copy.wait()


def limits(ident, megabytes=60):
    return pltpu.CompilerParams(
        collective_id=ident, has_side_effects=True, vmem_limit_bytes=megabytes * 1024 * 1024)


def attend(split, tok, fv, gains, square, wide, cosine, sine, prefix):
    seqs, rows, dim = tok.shape
    width = square[0].shape[1]
    heads = width // HEAD_DIM
    chunk = 64
    count = seqs * rows // chunk
    vmem = pl.BlockSpec(memory_space=pltpu.VMEM)
    anyw = pl.BlockSpec(memory_space=pl.ANY)
    dma = pltpu.SemaphoreType.DMA
    lines = pltpu.VMEM((count, chunk, dim), bf16)
    shape = jax.ShapeDtypeStruct
    full = [(dim, width)] * 3 + [(2, width, dim // 2)]
    outs = [
        shape((count, chunk, dim), bf16), shape((seqs, rows, width), bf16),
        shape((seqs, 4, 2, rows, width), bf16), shape((seqs, rows, width), bf16),
        shape((seqs, heads, rows), f32), shape((2, 8, dim // 2), f32)]
    out_specs = [anyw, vmem, anyw, vmem, vmem, vmem]
    scratch = []
    if split:
        outs += [shape(size, bf16) for size in full] + [shape(w.shape, bf16) for w in wide]
        out_specs += [anyw] * 7
        scratch = [pltpu.VMEM(size, bf16) for size in full] + [dma((7, 2)), dma((7, 2)), dma((4,)), dma((2,))]
    scratch += [
        pltpu.VMEM((seqs, rows, dim), bf16),
        pltpu.VMEM((seqs, 4, 2, rows, width), bf16),
        pltpu.VMEM((seqs, heads, width, rows), bf16),
        pltpu.VMEM((width, rows), bf16),
        pltpu.VMEM((width, rows), f32),
        pltpu.VMEM((heads, 1, rows), f32),
        pltpu.VMEM((heads, 1, rows), f32),
        lines, lines, lines, lines,
        dma((seqs, 3)), dma((seqs, 4)), dma((seqs,)),
        dma((count,)), dma((count,)), dma((count,)), dma((count,)), dma((count,)),
    ]
    return pl.pallas_call(
        functools.partial(attend_kernel, split),
        name="attend",
        out_shape=outs,
        in_specs=[vmem] * 8 + ([anyw] * 3 if split else []) + [vmem] * 2 + [pl.BlockSpec(memory_space=pltpu.SMEM)],
        out_specs=out_specs,
        scratch_shapes=scratch,
        compiler_params=limits(0),
        cost_estimate=pl.CostEstimate(flops=8 * 10**9, bytes_accessed=10**7, transcendentals=10**7),
    )(tok, fv, *gains, *square, *(wide if split else ()), cosine, sine, prefix)


def feed_kernel(split, *refs):
    place, ring, side = lax.axis_index("tp"), lax.axis_index("ctx"), lax.axis_index("fsdp")
    (tok, attn, cot, gains), refs = refs[:4], refs[4:]
    weights, refs = refs[: 6 if split else 3], refs[6 if split else 3 :]
    (mixed_hbm, late_hbm), saved, refs = refs[:2], refs[2:5], refs[5:]
    (wg, wu, wd, w_load, normed_t, inner_t, inner_s, gg, ug, late, part, inward, across, result,
     send_one, recv_one, send_two, recv_two, save, late_save), refs = refs[:20], refs[20:]
    (fold_d, fold_g, fold_u), (dwd, dwg, dwu) = make_folds(split, side, ring, refs, saved)
    seqs, rows, dim = tok.shape
    chunk = part.shape[1]
    tile = 256
    tiles = seqs * rows // tile
    early = tiles // 2
    per_tile = tile // chunk
    per_seq_tiles = rows // tile
    count = part.shape[0]
    loads = []
    for n, full in enumerate((wg, wu, wd)):
        if split:
            size = weights[n].shape[0]
            for m, owner in ((0, side), (1, 1 - side)):
                target = full.at[owner] if full.shape[0] == 2 else full.at[rows_at(owner * size, size)]
                loads.append(pltpu.make_async_copy(weights[n + 3 * m], target, w_load.at[n, m]))
        else:
            loads.append(pltpu.make_async_copy(weights[n], full, w_load.at[n, 0]))
    for load in loads:
        load.start()
    greet(line_peers(place) + (ring_peers(ring) + [{"fsdp": 1 - side}] if split else []))
    sums = Sum(place, part, inward, across, result, (send_one, recv_one, send_two, recv_two))
    gain_two = gain_row(gains, 1)
    middle = dim // 2

    def saving(i):
        return pltpu.make_async_copy(result.at[i], mixed_hbm.at[i], save.at[i])

    done = lambda i: saving(i).start()

    def saving_late(t):
        return pltpu.make_async_copy(late.at[t], late_hbm.at[t], late_save.at[t])

    for load in loads:
        load.wait()

    @pl.loop(0, tiles)
    def _(t):
        s, at = t // per_seq_tiles, rows_at(lax.rem(t, per_seq_tiles) * tile, tile)
        flat = rows_at(t * tile, tile)
        step_base = (t - 1) * per_tile

        def step(k):
            @pl.when(t > 0)
            def _():
                sums.step(step_base + k, done)

        hidden = tok[s, at, :].astype(f32) + attn[s, at, :].astype(f32)
        normed = (unit_norm(hidden) * gain_two).astype(bf16)
        normed_t[:, flat] = jnp.transpose(normed)
        gate = dot(normed, wg[...])
        up = dot(normed, wu[...])
        sigmoid = jax.nn.sigmoid(gate)
        swish = gate * sigmoid
        inner = (swish * up).astype(bf16)
        inner_s[...] = inner
        inner_t[:, flat] = jnp.transpose(inner)
        upstream = cot[s, at, :]
        inner_grad = dot_nt(upstream[:, :middle], wd[0]) + dot_nt(upstream[:, middle:], wd[1])
        gg[flat, :] = (inner_grad * up * sigmoid * (1.0 + gate * (1.0 - sigmoid))).astype(bf16)
        ug[flat, :] = (inner_grad * swish).astype(bf16)
        step(0)

        @pl.loop(0, per_tile)
        def _(k):
            own = rows_at(t * tile + k * chunk, chunk)
            i = jnp.where(t < early, 2 * per_tile * t, per_tile * (early + t)) + k
            part[i] = (dot_nt(gg[own, :], wg[...]) + dot_nt(ug[own, :], wu[...])).astype(bf16)
            sums.offer(i)

        step(1)

        @pl.when(t < early)
        def _():
            @pl.loop(0, per_tile)
            def _(k):
                i = 2 * per_tile * t + per_tile + k
                own = rows_at(k * chunk, chunk)
                for piece in range(2):
                    part[i, :, piece * middle : (piece + 1) * middle] = dot(inner_s[own, :], wd[piece]).astype(bf16)
                sums.offer(i)

        @pl.when(t >= early)
        def _():
            @pl.loop(0, per_tile)
            def _(k):
                own = rows_at(k * chunk, chunk)
                for piece in range(2):
                    late[t - early, own, piece * middle : (piece + 1) * middle] = dot(
                        inner_s[own, :], wd[piece]).astype(bf16)

            saving_late(t - early).start()

        step(2)
        step(3)

    begun = (tiles - 1) * per_tile
    deep, share = dwd.shape[2], dwg.shape[2]

    def wide_grad(target, right, first_step):
        @pl.loop(0, 4)
        def _(k):
            h, y = k // 2, lax.rem(k, 2)
            target[h, y] = dot(normed_t[rows_at((2 * y + h) * share, share), :], right[...]).astype(bf16)

            @pl.when(y == 1)
            def _():
                sums.step(first_step + h, done)

    for h in range(2):
        for y in range(2):
            total = jnp.zeros((deep, middle), f32)
            for s in range(seqs):
                total = total + dot(
                    inner_t[h * deep : (h + 1) * deep, s * rows : (s + 1) * rows],
                    cot[s, :, y * middle : (y + 1) * middle])
            dwd[h, y] = total.astype(bf16)
        sums.step(begun + h, done)
    fold_d.first()
    wide_grad(dwg, gg, begun + 2)
    fold_g.first()
    fold_d.second()
    wide_grad(dwu, ug, begun + 4)
    fold_u.first()
    fold_g.second()
    sums.step(begun + 6, done)
    fold_u.second()
    sums.step(begun + 7, done)
    fold_d.third()
    sums.step(begun + 8, done)
    fold_g.third()
    sums.step(begun + 9, done)
    fold_d.fourth()
    sums.step(begun + 10, done)
    fold_u.third()
    sums.step(begun + 11, done)
    fold_g.fourth()

    @pl.loop(begun + 12, count)
    def _(i):
        sums.step(i, done)

    sums.close(count, done)
    fold_u.fourth()
    folds = (fold_d, fold_g, fold_u)
    for fold in folds:
        fold.last()
    for fold in folds:
        fold.settle()
    for t in range(tiles - early):
        saving_late(t).wait()

    @pl.loop(0, count)
    def _(i):
        saving(i).wait()


def feed(split, tok, attn, cot, gains, weights, units):
    seqs, rows, dim = tok.shape
    chunk = 64
    tokens = seqs * rows
    count = tokens // chunk * 3 // 2
    vmem = pl.BlockSpec(memory_space=pltpu.VMEM)
    anyw = pl.BlockSpec(memory_space=pl.ANY)
    dma = pltpu.SemaphoreType.DMA
    lines = pltpu.VMEM((count, chunk, dim), bf16)
    tile = 256
    late = tokens // tile // 2
    shape = jax.ShapeDtypeStruct
    fold_scratch, fold_outs = fold_shapes(
        [(units // 2, dim // 2), (dim // 4, units), (dim // 4, units)], split)
    return pl.pallas_call(
        functools.partial(feed_kernel, split),
        name="feed",
        out_shape=[shape((count, chunk, dim), bf16), shape((late, tile, dim), bf16)] + fold_outs,
        in_specs=[vmem] * 4 + [anyw] * len(weights),
        out_specs=[anyw] * 5,
        scratch_shapes=[
            pltpu.VMEM((dim, units), bf16),
            pltpu.VMEM((dim, units), bf16),
            pltpu.VMEM((2, units, dim // 2), bf16),
            dma((3, 2)),
            pltpu.VMEM((dim, tokens), bf16),
            pltpu.VMEM((units, tokens), bf16),
            pltpu.VMEM((tile, units), bf16),
            pltpu.VMEM((tokens, units), bf16),
            pltpu.VMEM((tokens, units), bf16),
            pltpu.VMEM((late, tile, dim), bf16),
            lines, lines, lines, lines,
            dma((count,)), dma((count,)), dma((count,)), dma((count,)), dma((count,)), dma((late,)),
        ] + fold_scratch,
        compiler_params=limits(1),
        cost_estimate=pl.CostEstimate(flops=14 * 10**9, bytes_accessed=10**7, transcendentals=10**6),
    )(tok, attn, cot, gains, *weights)


def back_kernel(split, *refs):
    place, ring, side = lax.axis_index("tp"), lax.axis_index("ctx"), lax.axis_index("fsdp")
    (tok, attn, cot, mixed, late, gain_in, wq, wk, wv, wo, q, kv, ctx, lse, cosine, sine, prefix,
     block_hbm, token_hbm, fv_hbm, gain_out), saved, refs = refs[:21], refs[21:25], refs[25:]
    (hid, branch, qtm, qm, otm, om, kt, delta, dqt, dk, dv, give, take, proj, normed_t,
     part, inward, across, result, gain_part, gain_all,
     kv_send, kv_recv, send_one, recv_one, send_two, recv_two, save, fv_save, gain_send, gain_recv), refs = (
        refs[:31], refs[31:])
    (fold_o, fold_k, fold_v, fold_q), (dwo, dwk, dwv, dwq) = make_folds(split, side, ring, refs, saved)
    seqs, rows, dim = tok.shape
    width = wq.shape[1]
    heads = width // HEAD_DIM
    count, chunk = part.shape[0], part.shape[1]
    per_seq = rows // chunk
    tile = 256
    per_tile = tile // chunk
    middle = dim // 2
    mate, peer = ring_peers(ring)
    blocks = (ring, near(ring), lax.rem(ring + 2, 4), 3 - ring)
    others = [(dy, dc) for dy in range(2) for dc in range(4) if dy or dc]
    group = [{"fsdp": lax.rem(side + dy, 2), "ctx": lax.rem(ring + dc, 4)} for dy, dc in others]
    greet(line_peers(place) + (group if split else ring_peers(ring)))
    sums = Sum(place, part, inward, across, result, (send_one, recv_one, send_two, recv_two))
    gain_one, gain_two = gain_row(gain_in, 0), gain_row(gain_in, 1)
    gain_part[...] = jnp.zeros_like(gain_part)
    late_per = late.shape[1] // chunk

    @pl.loop(0, per_seq)
    def _(i):
        part[i] = late[i // late_per, rows_at(lax.rem(i, late_per) * chunk, chunk), :]
        sums.offer(i)

    def hidden_at(s, at):
        return tok[s, at, :].astype(f32) + attn[s, at, :].astype(f32)

    def chunk_of(n):
        return n // per_seq, rows_at(lax.rem(n, per_seq) * chunk, chunk)

    def saving_block(n):
        s, own = chunk_of(n)
        source = inward.at[n] if s == 0 else across.at[n - per_seq]
        return pltpu.make_async_copy(source, block_hbm.at[s, own], save.at[n])

    def saving_first(n):
        return pltpu.make_async_copy(inward.at[n], block_hbm.at[0, rows_at(n * chunk, chunk)], save.at[n])

    def saving_second(n):
        return pltpu.make_async_copy(
            across.at[n], block_hbm.at[1, rows_at(n * chunk, chunk)], save.at[per_seq + n])

    def saving_token(n):
        s, own = chunk_of(n)
        return pltpu.make_async_copy(across.at[per_seq + n], token_hbm.at[s, own], save.at[seqs * per_seq + n])

    def add_gain(which, value):
        for piece in range(2):
            gain_part[piece, which : which + 1, :] += value[:, piece * middle : (piece + 1) * middle]

    def done(i):
        @pl.when(i < per_seq)
        def _():
            across[i] = (hidden_at(1, rows_at(i * chunk, chunk)) + result[i].astype(f32)).astype(bf16)
            saving_second(i).start()

        @pl.when(i >= per_seq)
        def _():
            n = i - per_seq
            s, own = chunk_of(n)
            values, upstream = tok[s, own, :].astype(f32), result[i].astype(f32)
            factor = lax.rsqrt(jnp.mean(values * values, axis=-1, keepdims=True) + epsilon)
            scaled = upstream * gain_one
            add_gain(0, jnp.sum(upstream * values * factor, axis=0, keepdims=True))
            across[i] = (hid[s, own, :] + factor * scaled - values * factor**3 * jnp.mean(
                scaled * values, axis=-1, keepdims=True)).astype(bf16)
            saving_token(n).start()

    def move(s, source, target, device):
        return remote(give.at[source], take.at[s, target], kv_send.at[source], kv_recv.at[s, target], device)

    far_to_mate = lambda s: move(s, 2, 0, mate)
    peer_back = lambda s: move(s, 1, 1, peer)
    near_to_mate = lambda s: move(s, 0, 2, mate)

    for s in range(seqs):
        @pl.loop(0, rows // tile)
        def _(t):
            at = rows_at(t * tile, tile)
            values = hidden_at(s, at)
            n = s * (rows // tile) + t
            early = seqs * rows // tile // 2
            first = jnp.where(n < early, 2 * per_tile * n, per_tile * (early + n))
            upstream = jnp.concatenate([mixed[first + k] for k in range(per_tile)], axis=0).astype(f32)
            factor = lax.rsqrt(jnp.mean(values * values, axis=-1, keepdims=True) + epsilon)
            scaled = upstream * gain_two
            add_gain(1, jnp.sum(upstream * values * factor, axis=0, keepdims=True))
            hid_now = cot[s, at, :].astype(f32) + factor * scaled - values * factor**3 * jnp.mean(
                scaled * values, axis=-1, keepdims=True)
            hid[s, at, :] = hid_now
            low = hid_now.astype(bf16)
            branch[s, at, :] = low
            left, right = low[:, :middle], low[:, middle:]
            grad = dot_nt(left, wo[0]) + dot_nt(right, wo[1])
            lane_owner = lax.broadcasted_iota(jnp.int32, grad.shape, 1) // HEAD_DIM
            q_now = q[s, at, :].astype(f32)
            grad_t = dot_nt(wo[0], left) + dot_nt(wo[1], right)
            row_owner = lax.broadcasted_iota(jnp.int32, grad_t.shape, 0) // HEAD_DIM
            q_t = jnp.transpose(q_now)
            ctx_t = jnp.transpose(ctx[s, at, :].astype(f32))
            product = grad_t.astype(bf16).astype(f32) * ctx_t
            for h in range(heads):
                om[h, at, :] = jnp.where(lane_owner == h, grad, 0.0).astype(bf16)
                qm[h, at, :] = jnp.where(lane_owner == h, q_now, 0.0).astype(bf16)
                otm[h, :, at] = jnp.where(row_owner == h, grad_t, 0.0).astype(bf16)
                qtm[h, :, at] = jnp.where(row_owner == h, q_t, 0.0).astype(bf16)
                delta[h, :, at] = jnp.sum(
                    product[h * HEAD_DIM : (h + 1) * HEAD_DIM], axis=0, keepdims=True)
            normed = (unit_norm(tok[s, at, :].astype(f32)) * gain_one).astype(bf16)
            normed_t[:, rows_at(s * rows + t * tile, tile)] = jnp.transpose(normed)

        if s == seqs - 1:
            deep = dwo.shape[2]
            total = jnp.zeros((width, dim), f32)
            for r in range(seqs):
                total = total + dot(jnp.transpose(ctx[r]), branch[r])
            for h in range(2):
                for y in range(2):
                    dwo[h, y] = total[h * deep : (h + 1) * deep, y * middle : (y + 1) * middle].astype(bf16)
            fold_o.first()

        dqt[...] = jnp.zeros_like(dqt)

        def back_block(j, block_at, steps):
            kt[...] = jnp.transpose(kv[s, j, 0])
            key_pos = block_at * rows + lax.broadcasted_iota(jnp.int32, (rows, 1), 0)
            query_pos = ring * rows + lax.broadcasted_iota(jnp.int32, (1, rows), 1)
            seen = key_pos < jnp.maximum(query_pos + 1, prefix[s])
            dk[...] = jnp.zeros_like(dk)
            dv[...] = jnp.zeros_like(dv)

            @pl.loop(0, heads)
            def _(h):
                of_head = rows_at(h * HEAD_DIM, HEAD_DIM)
                scores = dot(kv[s, j, 0], qtm[h])
                probs = jnp.where(seen, jnp.exp(scores - lse[s, pl.ds(h, 1), :]), 0.0)
                dprobs = dot(kv[s, j, 1], otm[h])
                dv[...] += dot(probs.astype(bf16), om[h])
                dscores = (probs * (dprobs - delta[h])).astype(bf16)
                dk[...] += dot(dscores, qm[h])
                dqt[of_head, :] += dot(kt[of_head, :], dscores)

                @pl.when(lax.rem(h, 2) == 1)
                def _():
                    sums.step(steps + h // 2, done)

        base = s * per_seq
        last = s == seqs - 1
        back_block(3, blocks[3], base)
        if last:
            fold_o.second()
        if s > 0:
            far_to_mate(s - 1).wait_send()
        give[2, 0] = dk[...].astype(bf16)
        give[2, 1] = dv[...].astype(bf16)
        far_to_mate(s).start()
        back_block(2, blocks[2], base + 2)
        far_to_mate(s).wait_recv()
        if s > 0:
            peer_back(s - 1).wait_send()
        give[1, 0] = (dk[...] + take[s, 0, 0].astype(f32)).astype(bf16)
        give[1, 1] = (dv[...] + take[s, 0, 1].astype(f32)).astype(bf16)
        peer_back(s).start()
        back_block(1, blocks[1], base + 4)
        if last:
            fold_o.third()
        if s > 0:
            near_to_mate(s - 1).wait_send()
        give[0, 0] = dk[...].astype(bf16)
        give[0, 1] = dv[...].astype(bf16)
        near_to_mate(s).start()
        back_block(0, blocks[0], base + 6)
        near_to_mate(s).wait_recv()
        peer_back(s).wait_recv()

        @pl.loop(0, rows // tile)
        def _(t):
            at = rows_at(t * tile, tile)
            flat = rows_at(s * rows + t * tile, tile)
            co, si = cosine[at, :], sine[at, :]
            grad_v = 0.5 * (dv[at, :] + take[s, 2, 1, at, :].astype(f32) + take[s, 1, 1, at, :].astype(f32))
            grad_k = dk[at, :] + take[s, 2, 0, at, :].astype(f32) + take[s, 1, 0, at, :].astype(f32)
            grad_q = jnp.transpose(dqt[:, at]) * HEAD_DIM ** (-0.5)
            proj[0, flat, :] = (grad_q * co - turned(grad_q) * si).astype(bf16)
            proj[1, flat, :] = (grad_k * co - turned(grad_k) * si).astype(bf16)
            proj[2, flat, :] = grad_v.astype(bf16)

        @pl.loop(0, per_seq)
        def _(k):
            own = rows_at(s * rows + k * chunk, chunk)
            i = per_seq * (s + 1) + k
            part[i] = (
                dot_nt(proj[0, own, :], wq[...]) + dot_nt(proj[1, own, :], wk[...])
                + dot_nt(proj[2, own, :], wv[...])).astype(bf16)
            sums.offer(i)

    fv_copy = pltpu.make_async_copy(proj.at[2], fv_hbm, fv_save)
    fv_copy.start()
    share = dwq.shape[2]

    def square_grad(target, which):
        @pl.loop(0, 4)
        def _(k):
            h, y = k // 2, lax.rem(k, 2)
            target[h, y] = dot(normed_t[rows_at((2 * y + h) * share, share), :], proj[which]).astype(bf16)

    at_step = 2 * per_seq
    square_grad(dwk, 1)
    fold_k.first()
    sums.step(at_step, done)
    square_grad(dwv, 2)
    fold_v.first()
    fold_k.second()
    sums.step(at_step + 1, done)
    square_grad(dwq, 0)
    fold_q.first()
    fold_v.second()
    sums.step(at_step + 2, done)
    fold_q.second()
    fold_o.fourth()
    sums.step(at_step + 3, done)

    @pl.loop(0, per_seq)
    def _(i):
        own = rows_at(i * chunk, chunk)
        at = 2 * per_tile * (i // per_tile) + per_tile + lax.rem(i, per_tile)
        inward[i] = (hidden_at(0, own) + mixed[at].astype(f32)).astype(bf16)
        saving_first(i).start()

    fold_k.third()
    sums.step(at_step + 4, done)
    fold_v.third()
    sums.step(at_step + 5, done)
    fold_q.third()
    fold_k.fourth()
    sums.step(at_step + 6, done)
    fold_v.fourth()
    sums.step(at_step + 7, done)
    fold_q.fourth()

    @pl.loop(at_step + 8, count)
    def _(i):
        sums.step(i, done)

    sums.close(count, done)
    if split:
        me = 4 * side + ring
        gain_all[me] = gain_part[side]

        def share_gain(n):
            dy, dc = others[n]
            y = lax.rem(side + dy, 2)
            return remote(gain_part.at[y], gain_all.at[me], gain_send.at[n], gain_recv.at[n], group[n])

        for n in range(7):
            share_gain(n).start()
    folds = (fold_o, fold_k, fold_v, fold_q)
    for fold in folds:
        fold.last()
    if split:
        for n in range(7):
            share_gain(n).wait()
        total = gain_all[0]
        for n in range(1, 8):
            total = total + gain_all[n]
        gain_out[...] = total
    else:
        gain_out[...] = gain_part[...]
    for fold in folds:
        fold.settle()
    for copy in (far_to_mate, peer_back, near_to_mate):
        copy(seqs - 1).wait_send()
    fv_copy.wait()

    @pl.loop(0, per_seq)
    def _(i):
        saving_first(i).wait()
        saving_second(i).wait()

    @pl.loop(0, seqs * per_seq)
    def _(i):
        saving_token(i).wait()


def back(split, tok, attn, cot, mixed, late, gains, square, q, kv, ctx, lse, cosine, sine, prefix):
    seqs, rows, dim = tok.shape
    width = q.shape[2]
    heads = width // HEAD_DIM
    count, chunk, _ = mixed.shape
    tokens = seqs * rows
    vmem = pl.BlockSpec(memory_space=pltpu.VMEM)
    anyw = pl.BlockSpec(memory_space=pl.ANY)
    dma = pltpu.SemaphoreType.DMA
    lines = pltpu.VMEM((count, chunk, dim), bf16)
    wide = pltpu.VMEM((heads, rows, width), bf16)
    tall = pltpu.VMEM((heads, width, rows), bf16)
    shape = jax.ShapeDtypeStruct
    fold_scratch, fold_outs = fold_shapes([(width // 2, dim // 2)] + [(dim // 4, width)] * 3, split)
    return pl.pallas_call(
        functools.partial(back_kernel, split),
        name="back",
        out_shape=[
            shape((seqs, rows, dim), bf16), shape((seqs, rows, dim), bf16), shape((tokens, width), bf16),
            shape((8, dim // 2) if split else (2, 8, dim // 2), f32)] + fold_outs,
        in_specs=[vmem] * 16 + [pl.BlockSpec(memory_space=pltpu.SMEM)],
        out_specs=[anyw, anyw, anyw, vmem] + [anyw] * 4,
        scratch_shapes=[
            pltpu.VMEM((seqs, rows, dim), f32),
            pltpu.VMEM((seqs, rows, dim), bf16),
            tall, wide, tall, wide,
            pltpu.VMEM((width, rows), bf16),
            pltpu.VMEM((heads, 1, rows), f32),
            pltpu.VMEM((width, rows), f32),
            pltpu.VMEM((rows, width), f32),
            pltpu.VMEM((rows, width), f32),
            pltpu.VMEM((3, 2, rows, width), bf16),
            pltpu.VMEM((seqs, 3, 2, rows, width), bf16),
            pltpu.VMEM((3, tokens, width), bf16),
            pltpu.VMEM((dim, tokens), bf16),
            lines, lines, lines, lines,
            pltpu.VMEM((2, 8, dim // 2), f32),
            pltpu.VMEM((8, 8, dim // 2), f32),
            dma((3,)), dma((seqs, 3)),
            dma((count,)), dma((count,)), dma((count,)), dma((count,)), dma((2 * tokens // chunk,)),
            dma(()), dma((7,)), dma((7,)),
        ] + fold_scratch,
        compiler_params=limits(2, 62),
        cost_estimate=pl.CostEstimate(flops=30 * 10**9, bytes_accessed=10**7, transcendentals=10**7),
    )(tok, attn, cot, mixed, late, gains, *square, q, kv, ctx, lse, cosine, sine, prefix)


def rope_tables(positions, lanes):
    half_dim = HEAD_DIM // 2
    lane = jnp.arange(lanes, dtype=jnp.int32) % HEAD_DIM
    frequency = rope_base ** (-(lane % half_dim).astype(f32) / half_dim)
    angles = positions.astype(f32)[:, None] * frequency[None, :]
    return jnp.cos(angles), jnp.sin(angles) * jnp.where(lane < half_dim, -1.0, 1.0)


def halves(weight):
    rows, columns = weight.shape
    return jnp.swapaxes(weight.reshape(rows, 2, columns // 2), 0, 1)


def shards(
    tokens, first_values, norm1_gain, norm2_gain, w_query, w_key, w_value, w_out, w_gate, w_up, w_down,
    prefix, cotangent,
):
    split = lax.axis_size("fsdp") == 2
    seqs, rows, dim = tokens.shape
    width, units = w_query.shape[1], w_gate.shape[1]
    positions = lax.axis_index("ctx") * rows + jnp.arange(rows, dtype=jnp.int32)
    cosine, sine = rope_tables(positions, width)
    gather = functools.partial(lax.all_gather, axis_name="fsdp", tiled=True)
    if split:
        gains = (norm1_gain[None, :], norm2_gain[None, :])
        square = (w_query, w_key, w_value, w_out)
        wide = (w_gate, w_up, w_down)
    else:
        gains = (gather(norm1_gain)[None, :], gather(norm2_gain)[None, :])
        square = (gather(w_query), gather(w_key), gather(w_value), halves(gather(w_out, axis=1)))
        wide = (gather(w_gate), gather(w_up), halves(gather(w_down, axis=1)))
    attn_sum, query, pairs, context, log_total, gain_rows, *gathered = attend(
        split, tokens, first_values, gains, square, wide, cosine, sine, prefix)
    if split:
        square = tuple(gathered[:4])
        wide = wide + tuple(gathered[4:])
    attn_sum = attn_sum.reshape(tokens.shape)
    mixed, late, down_grad, gate_grad, up_grad = feed(
        split, tokens, attn_sum, cotangent, gain_rows, wide, units)
    block_out, token_grad, half_value_grad, gain_grads, out_grad, key_grad, value_grad, query_grad = back(
        split, tokens, attn_sum, cotangent, mixed, late, gain_rows, square, query, pairs, context,
        log_total, cosine, sine, prefix)
    if split:
        over_rows = lambda grad: grad.reshape(-1, grad.shape[-1]).astype(f32)
        over_columns = over_rows
        gain_one_grad, gain_two_grad = gain_grads[0], gain_grads[1]
    else:
        total = lambda grad, axis: lax.psum(
            lax.psum_scatter(grad, "fsdp", scatter_dimension=axis, tiled=True), "ctx").astype(f32)
        over_rows = lambda grad: total(jnp.swapaxes(grad, 0, 1).reshape(-1, grad.shape[-1]), 0)
        over_columns = lambda grad: total(
            jnp.transpose(grad, (0, 2, 1, 3)).reshape(2 * grad.shape[2], -1), 1)
        gain_one_grad, gain_two_grad = (total(gain_grads[:, n].reshape(-1), 0) for n in range(2))
    return (
        block_out,
        token_grad.astype(f32),
        half_value_grad.reshape(seqs, rows, width).astype(f32),
        gain_one_grad,
        gain_two_grad,
        over_rows(query_grad),
        over_rows(key_grad),
        over_rows(value_grad),
        over_columns(out_grad),
        over_rows(gate_grad),
        over_rows(up_grad),
        over_columns(down_grad),
    )


def solution(mesh):
    return jax.shard_map(
        shards,
        mesh=mesh,
        in_specs=(
            P("fsdp", "ctx", None),
            P("fsdp", "ctx", "tp"),
            P("fsdp"),
            P("fsdp"),
            P("fsdp", "tp"),
            P("fsdp", "tp"),
            P("fsdp", "tp"),
            P("tp", "fsdp"),
            P("fsdp", "tp"),
            P("fsdp", "tp"),
            P("tp", "fsdp"),
            P("fsdp"),
            P("fsdp", "ctx", None),
        ),
        out_specs=(
            P("fsdp", "ctx", None),
            P("fsdp", "ctx", None),
            P("fsdp", "ctx", "tp"),
            P("fsdp"),
            P("fsdp"),
            P("fsdp", "tp"),
            P("fsdp", "tp"),
            P("fsdp", "tp"),
            P("tp", "fsdp"),
            P("fsdp", "tp"),
            P("fsdp", "tp"),
            P("tp", "fsdp"),
        ),
        check_vma=False,
    )
```

time: 605 us -> 356 us (0.59)
  waiting for transfers between devices: 210 us -> 0 us
  blocking collectives: 63.2 us -> 0 us
  Pallas kernels: 293 us -> 319 us
  between operations: 14.8 us -> 1.16 us
  other arithmetic: 8.2 us -> 16.2 us
    reduce_scatter x7 -> x0, waiting for transfers between devices: 143 us -> none  [the longest x1 28.4 us: shards(): lax.psum_scatter(up_weight_grad.astype(jnp.bfloat16), 'fsdp', scatter_dim...]
    psum x1 -> x0, waiting for transfers between devices: 62.3 us -> none  [shards(): lax.psum(sum_gate.astype(jnp.bfloat16), 'ctx').astype(jnp.float32)]
    all_gather x6 -> x0, blocking collectives: 52.2 us -> none  [the longest x1 12.6 us: shards(): lax.all_gather(w_key, 'fsdp', axis=0, tiled=True)]
    pallas_call x3, Pallas kernels: 293 us -> 319 us  [the longest x1 119 us: back(): pl.pallas_call(functools.partial(back_kernel, split), name='back', out_sh...]
    convert_element_type x8 -> x10, other arithmetic: 7.03 us -> 13.2 us  [the longest x7 7.93 us: shards(): over_rows = lambda grad: grad.reshape(-1, grad.shape[-1]).astype(f32)]
    unnamed x48 -> x17, local copies, waits for them, and re-layouts: 13 us -> 8.98 us
  transfers between devices with their start and end apart: 11 -> 0, of which waited for: 8 -> 0; matrix products, arithmetic and copies ran while one was open for 1% -> 0% of each run, Pallas kernels for 14% -> 0%
where the time goes in v2:
time: 356 us; the launch traced here: 349 us
  Pallas kernels  319 us (90%)
  other arithmetic  16.2 us (5%)
  local copies, waits for them, and re-layouts  12.9 us (4%)
    pallas_call x1, Pallas kernels, back(): pl.pallas_call(functools.partial(back_kernel, split), name='back', out_sh...  119 us
    pallas_call x1, Pallas kernels, feed(): pl.pallas_call(functools.partial(feed_kernel, split), name='feed', out_sh...  101 us
    pallas_call x1, Pallas kernels, attend(): pl.pallas_call(functools.partial(attend_kernel, split), name='attend', ou...  99.3 us
    unnamed x17, local copies, waits for them, and re-layouts  8.98 us
    convert_element_type x7, other arithmetic, shards(): over_rows = lambda grad: grad.reshape(-1, grad.shape[-1]).astype(f32)  7.93 us

profile of v2, /device:TPU:0, one launch (start us, length us, event | category | flops | bytes accessed | tf_op | source)
XLA Modules:
  0.0 349.5 jit_solution(12246794705319847836)
XLA Ops:
  0.7 1.3 broadcast_in_dim.17.refs_2_
  1.9 1.3 broadcast_in_dim.18.refs_3_
  3.2 2.3 copy.25.refs_8_.refs_4_
  5.5 2.3 copy.26.refs_9_.refs_5_
  7.7 3.0 fusion
  10.8 99.3 %attend.1 = (bf16[16,64,1024]{2,1,0:T(8,128)(2,1)}, bf16[2,512,256]{2,1,0:T(8,128)(2,1)}, bf16[2,4,2,512,256]{4,3,2,1,0:T(8,128)(2,1)}, bf16[2,512,256]{2,1,0:T(...) custom-call(bf16[2,512,1024]{2,1,0:T(8,128)(2,1)} %refs_0_.5, ...), custom_call_target="tpu_custom_call" | custom-call | flops 8000000000 | bytes 10000000 | tf_op jit(solution)/shard_map/attend/pallas_call | solution.py:502
  110.1 101.0 %feed.1 = (bf16[24,64,1024]{2,1,0:T(8,128)(2,1)}, bf16[2,256,1024]{2,1,0:T(8,128)(2,1)}, bf16[2,352,512]{2,1,0:T(8,128)(2,1)}, bf16[2,256,704]{2,1,0:T(8,128)(2,1)}, bf16[2,256,704]{2,1,0:T(8,128)(2,1)}) custom-call(bf16[2,512,1024]{2,1,0:T(8,128)(2,1)} %refs_0_.5, bf16[2,512,1024]{2,1,0:T(8,128)(2,1)} %bitcast.29, bf16[2,512,1024]{2,1,0:T(8,128)(2,1)} %refs_2_.3, ...), custom_call_target="tpu_custom_call" | custom-call | flops 14000000000 | bytes 10000000 | tf_op jit(solution)/shard_map/feed/pallas_call | solution.py:692
  211.2 118.8 %back.1 = (bf16[2,512,1024]{2,1,0:T(8,128)(2,1)}, bf16[2,512,1024]{2,1,0:T(8,128)(2,1)}, bf16[1024,256]{1,0:T(8,128)(2,1)}, f32[8,512]{1,0:T(8,128)}, bf16[2,128...) custom-call(bf16[2,512,1024]{2,1,0:T(8,128)(2,1)} %refs_0_.5, ...), custom_call_target="tpu_custom_call" | custom-call | flops 30000001024 | bytes 10000000 | tf_op jit(solution)/shard_map/back/pallas_call | solution.py:1023
  330.0 0.0 copy-start.5
  330.0 0.0 copy-start.4
  330.0 1.4 fusion.6
  331.4 1.8 bitcast_convert_fusion.6
  333.2 0.0 copy-start.3
  333.2 1.8 bitcast_convert_fusion.5
  335.0 1.8 bitcast_convert_fusion.4
  336.8 0.0 copy-done.5
  336.8 0.0 copy-start.2
  336.8 0.9 bitcast_convert_fusion.3
  337.7 0.0 copy-done.4
  337.7 1.0 convert.8
  338.7 0.0 copy-done.3
  338.7 1.3 bitcast_convert_fusion.2
  340.1 0.0 copy-done.2
  340.1 0.0 copy-start.1
  340.1 0.2 bitcast_convert_fusion.1
  340.2 1.6 copy.29
  341.8 0.0 copy-done.1
  341.8 0.2 bitcast_convert_fusion
  341.9 1.6 copy.30
  343.5 4.2 %convert_element_type.67 = f32[2,512,1024]{2,1,0:T(8,128)} convert(bf16[2,512,1024]{2,1,0:T(8,128)(2,1)} %get-tuple-element.54) | non-fusion elementwise | flops 1048576 | bytes 6291456 | tf_op jit(solution)/shard_map/convert_element_type | solution.py:1111
  347.7 0.0 copy-done
  347.7 1.3 copy.32
  (3 shorter events, 0.0 us)
Async XLA Ops:
  330.0 6.8 %copy-start.5 = (bf16[2,128,512]{2,1,0:T(8,128)(2,1)S(1)}, bf16[2,128,512]{2,1,0:T(8,128)(2,1)}, u32[]{:S(2)}) copy-start(bf16[2,128,512]{2,1,0:T(8,128)(2,1)} %get-tuple-element.60) | copy-start | bytes 786436
  330.0 7.7 %copy-start.4 = (bf16[1024,256]{1,0:T(8,128)(2,1)S(1)}, bf16[1024,256]{1,0:T(8,128)(2,1)}, u32[]{:S(2)}) copy-start(bf16[1024,256]{1,0:T(8,128)(2,1)} %get-tuple-element.55) | copy-start | bytes 1572868
  333.2 5.6 %copy-start.3 = (bf16[2,352,512]{2,1,0:T(8,128)(2,1)S(1)}, bf16[2,352,512]{2,1,0:T(8,128)(2,1)}, u32[]{:S(2)}) copy-start(bf16[2,352,512]{2,1,0:T(8,128)(2,1)} %get-tuple-element.63) | copy-start | bytes 2162692
  336.8 3.3 copy-start.2
  340.1 1.7 copy-start.1
  343.5 4.2 %copy-start = (bf16[2,512,1024]{2,1,0:T(8,128)(2,1)S(1)}, bf16[2,512,1024]{2,1,0:T(8,128)(2,1)}, u32[]{:S(2)}) copy-start(bf16[2,512,1024]{2,1,0:T(8,128)(2,1)} %get-tuple-element.94) | copy-start | bytes 6291460
